TPU v7x, 128 devices: a whole 4x4x4 slice. The times are simulated.
128 devices in a mesh: blk: 8 (over x, y_lo), dom: 16 (over z, y_hi, core).
Axes of the slice: x: 4, y: 4 (y_hi: 2, y_lo: 2; y = y_hi * 2 + y_lo), z: 4, core: 2. Of those that a mesh axis runs over, the one named last changes fastest.
Arguments:
- positions: float32 [3, 131072], P(None, ('blk', 'dom')), may hold values from -6 to 6
- line_vectors: float32 [3, 131072], P(None, ('blk', 'dom')), may hold values from -6 to 6
- burgers: float32 [3, 131072], P(None, ('blk', 'dom')), may hold values from -6 to 6
- mobility: float32 [131072], P(('blk', 'dom')), may hold values from 0.5 to 2
- close_list: int32 [32, 131072], P(None, ('blk', 'dom')), may hold values from 0 to 256, as said below
- ghost_map: int32 [4, 65536], P(None, ('blk', 'dom')), may hold values from 0 to 1023, as said below
Outputs:
- new_positions: float32 [3, 131072], P(None, ('blk', 'dom'))
- velocity: float32 [3, 131072], P(None, ('blk', 'dom'))
Inputs may be any that keep to these rules, and one draw needn't show every extreme that they name: `close_list`: each entry is a place in the window of the segment's cell: below 128 a segment of the same cell, 128 + u the u-th row of the cell's ghost window, and 256 an empty slot. `ghost_map`: for each subcycle, each device's run of 512 entries holds first 256 distinct local segment numbers below 512 (the ghosts of the lower domain), the first of them 0, then 256 distinct local numbers of at least 1024 - 512 (the ghosts of the upper domain), the first of them 1024 - 1.
All inputs are finite; a program needn't handle non-finite values.
Results may differ from a plain program's by a relative error of at most 0.0005.
Values sent between devices are 32-bit elements; how exact they have to be, the bound alone decides.
A program may use at most 64 MiB of HBM per device.

v0:
```python
import math

import jax
import jax.numpy as jnp
from jax import lax
from jax.sharding import PartitionSpec as P

CELL_SEGS = 128
SLOTS = 32
GHOSTS = 256
SUBS = 4
RIM_ROWS = 512


long_core = 1.0
short_core = 0.25
time_step = 0.05


def shifted(value, axis, steps):
    count = lax.axis_size(axis)
    pairs = [(source, (source + steps) % count) for source in range(count)]
    return lax.ppermute(value, axis, pairs)


def extended(cells, sides, width):
    for axis, dim in sides:
        count = lax.axis_size(axis)
        head = lax.slice_in_dim(cells, 0, width, axis=dim)
        tail = lax.slice_in_dim(cells, cells.shape[dim] - width, cells.shape[dim], axis=dim)
        cells = jnp.concatenate(
            [
                lax.ppermute(tail, axis, [(i, (i + 1) % count) for i in range(count)]),
                cells,
                lax.ppermute(head, axis, [((i + 1) % count, i) for i in range(count)]),
            ],
            axis=dim,
        )
    return cells


def pair_weights(target, source, core):
    delta_x = target[0][..., :, None] - source[0][..., None, :]
    delta_y = target[1][..., :, None] - source[1][..., None, :]
    delta_z = target[2][..., :, None] - source[2][..., None, :]
    radius = delta_x * delta_x + delta_y * delta_y + delta_z * delta_z + core * core
    inverse = lax.rsqrt(radius)
    line_dot = (
        target[3][..., :, None] * source[3][..., None, :]
        + target[4][..., :, None] * source[4][..., None, :]
        + target[5][..., :, None] * source[5][..., None, :]
    )
    burgers_dot = (
        target[6][..., :, None] * source[6][..., None, :]
        + target[7][..., :, None] * source[7][..., None, :]
        + target[8][..., :, None] * source[8][..., None, :]
    )
    weight = burgers_dot * line_dot * inverse * inverse * inverse
    return (weight, (delta_x, delta_y, delta_z))


def cell_force(target, source):
    weight, deltas = pair_weights(target, source, long_core)
    return jnp.stack([jnp.sum(weight * delta, axis=-1) for delta in deltas])


def as_cells(rows):
    return rows.reshape(rows.shape[0], -1, CELL_SEGS)


def flatten_cells(cell_rows):
    return cell_rows.reshape(cell_rows.shape[0], -1)


def slot_force(own_rows, partners):
    delta_x = own_rows[0][None] - partners[0]
    delta_y = own_rows[1][None] - partners[1]
    delta_z = own_rows[2][None] - partners[2]
    radius = delta_x * delta_x + delta_y * delta_y + delta_z * delta_z + short_core * short_core
    inverse = lax.rsqrt(radius)
    line_dot = (
        own_rows[3][None] * partners[3]
        + own_rows[4][None] * partners[4]
        + own_rows[5][None] * partners[5]
    )
    burgers_dot = (
        own_rows[6][None] * partners[6]
        + own_rows[7][None] * partners[7]
        + own_rows[8][None] * partners[8]
    )
    weight = burgers_dot * line_dot * inverse * inverse * inverse
    return jnp.stack(
        [jnp.sum(weight * delta_x, 0), jnp.sum(weight * delta_y, 0), jnp.sum(weight * delta_z, 0)]
    )


def local(positions, line_vectors, burgers, mobility, close_list, ghost_map):
    seg_count = positions.shape[1]
    statics = jnp.concatenate([line_vectors, burgers], 0)
    seg_state = jnp.concatenate([positions, statics], 0)
    cell_rows = as_cells(seg_state)
    blocks = lax.axis_size("blk")
    cycle_reach = blocks // 4
    forces = cell_force(cell_rows, cell_rows)
    upward = seg_state
    downward = seg_state
    for offset in range(cycle_reach):
        upward = shifted(upward, "blk", 1)
        downward = shifted(downward, "blk", -1)
        forces = (
            forces
            + cell_force(cell_rows, as_cells(upward))
            + cell_force(cell_rows, as_cells(downward))
        )
    long_force = flatten_cells(forces) * (1.0 / math.sqrt((2 * cycle_reach + 1) * CELL_SEGS))
    window_count = 2 * GHOSTS // CELL_SEGS
    seg_index = jnp.arange(seg_count, dtype=jnp.int32)
    cell_index = seg_index // CELL_SEGS
    own_place = cell_index[None, :] * CELL_SEGS + close_list
    ghost_place = (
        seg_count + cell_index[None, :] % window_count * CELL_SEGS + (close_list - CELL_SEGS)
    )
    empty_place = seg_count + 2 * GHOSTS
    places = jnp.where(
        close_list < CELL_SEGS,
        own_place,
        jnp.where(close_list < 2 * CELL_SEGS, ghost_place, empty_place),
    )
    near_maps = extended(ghost_map, (("dom", 1),), GHOSTS)

    def ghost_rows_of(current, subcycle):
        full_rows = jnp.concatenate([current, statics], 0)
        rim_rows = extended(full_rows, (("dom", 1),), RIM_ROWS)
        lower_index = near_maps[subcycle, :GHOSTS] - (seg_count - RIM_ROWS)
        upper_index = near_maps[subcycle, 3 * GHOSTS :]
        from_lower = jnp.take(rim_rows[:, :RIM_ROWS], lower_index, axis=1)
        from_upper = jnp.take(rim_rows[:, RIM_ROWS + seg_count :], upper_index, axis=1)
        return (full_rows, jnp.concatenate([from_lower, from_upper], 1))

    def short_force(full_rows, ghost_rows):
        extended_rows = jnp.concatenate([full_rows, ghost_rows], 1)
        partners = jnp.take(extended_rows, places, axis=1, mode="fill", fill_value=0.0)
        return slot_force(full_rows, partners) * (1.0 / math.sqrt(SLOTS))

    velocity = jnp.zeros_like(positions)
    for subcycle in range(SUBS):
        full_rows, ghost_rows = ghost_rows_of(positions, subcycle)
        first_vel = mobility * (long_force + short_force(full_rows, ghost_rows))
        guess_pos = positions + time_step * first_vel
        full_rows, ghost_rows = ghost_rows_of(guess_pos, subcycle)
        second = mobility * (long_force + short_force(full_rows, ghost_rows))
        velocity = 0.5 * (first_vel + second)
        positions = positions + time_step * velocity
    return (positions, velocity)


def solution(mesh):
    return jax.shard_map(
        local,
        mesh=mesh,
        in_specs=(
            P(None, ("blk", "dom")),
            P(None, ("blk", "dom")),
            P(None, ("blk", "dom")),
            P(("blk", "dom")),
            P(None, ("blk", "dom")),
            P(None, ("blk", "dom")),
        ),
        out_specs=(P(None, ("blk", "dom")), P(None, ("blk", "dom"))),
        check_vma=False,
    )
```

profile of v0, /device:TPU:1, one launch (start us, length us, event | category | flops | bytes accessed | tf_op | source)
XLA Modules:
  0.0 1072.2 jit_solution(9508008211150095777)
XLA Ops:
  0.6 0.8 pad_maximum_fusion.15
  1.4 4.4 collective-permute-start.1
  6.5 3.5 collective-permute-start.5
  10.7 0.8 fusion.206
  11.6 0.8 fusion.207
  12.4 1.0 fusion.147
  13.4 1.0 compare_and_fusion
  14.8 2.7 collective-permute-start.6
  18.7 3.5 collective-permute-done.6
  23.1 108.2 %gather_fusion.2 = f32[32768,9]{1,0:T(8,128)} fusion(f32[9,1536]{0,1:T(8,128)S(1)} %pad_maximum_fusion, s32[32768]{0:T(1024)S(1)} %broadcast_clamp_fusion), kind=kCustom, calls=%fused_computation.1.clone | custom fusion | bytes 2490368 | tf_op jit(solution)/shard_map/jit(_take)/gather | solution.py:142
  131.3 10.0 copy.163
  141.8 2.2 fusion.11
  144.0 3.3 collective-permute-start.3
  147.3 2.2 fusion.18
  149.6 2.6 fusion.32
  152.3 2.5 collective-permute-done.2
  154.8 2.2 fusion.25
  157.3 1.9 collective-permute-start.8
  159.7 2.8 collective-permute-done.8
  163.4 5.3 collective-permute-done.9
  169.6 108.2 %gather_fusion.5 = f32[32768,9]{1,0:T(8,128)} fusion(f32[9,1536]{0,1:T(8,128)S(1)} %pad_maximum_fusion.1, s32[32768]{0:T(1024)S(1)} %broadcast_clamp_fusion), kind=kCustom, calls=%fused_computation.17.clone | custom fusion | bytes 2490368 | tf_op jit(solution)/shard_map/jit(_take)/gather | solution.py:142
  277.8 10.0 copy.167
  288.9 0.8 collective-permute-start.11
  289.7 2.2 collective-permute-done.10
  292.7 6.9 collective-permute-done.11
  300.4 108.2 %gather_fusion.8 = f32[32768,9]{1,0:T(8,128)} fusion(f32[9,1536]{0,1:T(8,128)S(1)} %pad_maximum_fusion.2, s32[32768]{0:T(1024)S(1)} %broadcast_clamp_fusion), kind=kCustom, calls=%fused_computation.18.clone | custom fusion | bytes 2490368 | tf_op jit(solution)/shard_map/jit(_take)/gather | solution.py:142
  408.7 10.0 copy.171
  419.7 1.7 collective-permute-start.13
  421.4 1.2 collective-permute-done.12
  423.5 5.8 collective-permute-done.13
  430.1 108.2 %gather_fusion.11 = f32[32768,9]{1,0:T(8,128)} fusion(f32[9,1536]{0,1:T(8,128)S(1)} %pad_maximum_fusion.3, s32[32768]{0:T(1024)S(1)} %broadcast_clamp_fusion), kind=kCustom, calls=%fused_computation.19.clone | custom fusion | bytes 2490368 | tf_op jit(solution)/shard_map/jit(_take)/gather | solution.py:142
  538.4 10.0 copy.175
  549.4 3.9 collective-permute-start.15
  554.7 4.9 collective-permute-done.15
  560.5 108.2 %gather_fusion.14 = f32[32768,9]{1,0:T(8,128)} fusion(f32[9,1536]{0,1:T(8,128)S(1)} %pad_maximum_fusion.4, s32[32768]{0:T(1024)S(1)} %broadcast_clamp_fusion), kind=kCustom, calls=%fused_computation.20.clone | custom fusion | bytes 2490368 | tf_op jit(solution)/shard_map/jit(_take)/gather | solution.py:142
  668.7 10.0 copy.179
  679.8 5.2 collective-permute-start.17
  686.4 3.7 collective-permute-done.17
  691.1 108.2 %gather_fusion.17 = f32[32768,9]{1,0:T(8,128)} fusion(f32[9,1536]{0,1:T(8,128)S(1)} %pad_maximum_fusion.5, s32[32768]{0:T(1024)S(1)} %broadcast_clamp_fusion), kind=kCustom, calls=%fused_computation.21.clone | custom fusion | bytes 2490368 | tf_op jit(solution)/shard_map/jit(_take)/gather | solution.py:142
  799.3 10.0 copy.183
  810.4 6.6 collective-permute-start.19
  818.4 2.2 collective-permute-done.19
  821.5 108.2 %gather_fusion.20 = f32[32768,9]{1,0:T(8,128)} fusion(f32[9,1536]{0,1:T(8,128)S(1)} %pad_maximum_fusion.6, s32[32768]{0:T(1024)S(1)} %broadcast_clamp_fusion), kind=kCustom, calls=%fused_computation.22.clone | custom fusion | bytes 2490368 | tf_op jit(solution)/shard_map/jit(_take)/gather | solution.py:142
  929.7 10.0 copy.187
  940.7 8.0 collective-permute-start.21
  950.1 1.3 collective-permute-done.21
  952.3 108.2 %gather_fusion.23 = f32[32768,9]{1,0:T(8,128)} fusion(f32[9,1536]{0,1:T(8,128)S(1)} %pad_maximum_fusion.7, s32[32768]{0:T(1024)S(1)} %broadcast_clamp_fusion), kind=kCustom, calls=%fused_computation.23.clone | custom fusion | bytes 2490368 | tf_op jit(solution)/shard_map/jit(_take)/gather | solution.py:142
  1060.5 10.0 copy.191
  (175 shorter events, 26.6 us)
Async XLA Ops:
  0.6 13.8 %copy-start.3 = (f32[3,1024]{1,0:T(4,128)S(1)}, f32[3,1024]{1,0:T(4,128)}, u32[]{:S(2)}) copy-start(f32[3,1024]{1,0:T(4,128)} %param.10) | copy-start | bytes 36868
  1.4 142.5 %collective-permute-start.1 = (f32[9,1024]{1,0:T(8,128)S(1)}, f32[9,1024]{1,0:T(8,128)S(1)}, u32[]{:S(2)}, u32[]{:S(2)}) collective-permute-start(f32[9,1024]{1,0:T(8,128)S(1)} %pad_maximum_fusion.15), channel_id=1, source_target_pairs={{0,112},{16,0},{32,16},{48,32},{64,48},{80,64},{96,80},{112,96},{1... | collective-permute-start | bytes 110600 | tf_op jit(solution)/shard_map/ppermute | solution.py:23
  5.8 135.9 %collective-permute-start = (f32[9,1024]{1,0:T(8,128)S(1)}, f32[9,1024]{1,0:T(8,128)S(1)}, u32[]{:S(2)}, u32[]{:S(2)}) collective-permute-start(f32[9,1024]{1,0:T(8,128)S(1)} %pad_maximum_fusion.15), channel_id=1, source_target_pairs={{0,16},{16,32},{32,48},{48,64},{64,80},{80,96},{96,112},{112,0},{1... | collective-permute-start | bytes 110600 | tf_op jit(solution)/shard_map/ppermute | solution.py:23
  6.5 8.3 collective-permute-start.5
  10.1 7.7 collective-permute-start.4
  10.2 7.3 collective-permute-start.7
  14.8 7.4 collective-permute-start.6
  141.7 15.3 %copy-start.2 = (f32[1024]{0:T(1024)S(1)}, f32[1024]{0:T(1024)}, u32[]{:S(2)}) copy-start(f32[1024]{0:T(1024)} %param.13) | copy-start | bytes 12292
  141.7 15.4 %copy-start = (f32[3,1024]{1,0:T(4,128)S(1)}, f32[3,1024]{1,0:T(4,128)}, u32[]{:S(2)}) copy-start(f32[3,1024]{1,0:T(4,128)} %param.12) | copy-start | bytes 36868
  141.7 15.4 %copy-start.1 = (f32[3,1024]{1,0:T(4,128)S(1)}, f32[3,1024]{1,0:T(4,128)}, u32[]{:S(2)}) copy-start(f32[3,1024]{1,0:T(4,128)} %param.11) | copy-start | bytes 36868
  144.0 5.6 collective-permute-start.3
  149.5 5.3 collective-permute-start.2
  157.3 5.3 collective-permute-start.8
  159.7 9.1 collective-permute-start.9
  288.4 3.4 collective-permute-start.10
  288.9 10.6 collective-permute-start.11
  419.2 3.4 collective-permute-start.12
  419.7 9.5 collective-permute-start.13
  549.0 4.9 collective-permute-start.14
  549.4 10.2 collective-permute-start.15
  679.3 6.3 collective-permute-start.16
  679.8 10.4 collective-permute-start.17
  809.9 7.6 collective-permute-start.18
  810.4 10.2 collective-permute-start.19
  940.3 9.0 collective-permute-start.20
  940.7 10.7 collective-permute-start.21
where the time goes:
time: 1080 us; the launch traced here: 1070 us
  local copies, waits for them, and re-layouts  964 us (89%)
  waiting for transfers between devices  44.6 us (4%)
  starting transfers between devices  43.1 us (4%)
  other arithmetic  18.4 us (2%)
    gather x16, local copies, waits for them, and re-layouts, short_force(): jnp.take(extended_rows, places, axis=1, mode='fill', fill_value=0.0)  946 us
    ppermute x9, waiting for transfers between devices, extended(): lax.ppermute(head, axis, [((i + 1) % count, i) for i in range(count)])  33.6 us
    ppermute x9, starting transfers between devices, extended(): lax.ppermute(head, axis, [((i + 1) % count, i) for i in range(count)])  29.4 us
  transfers between devices with their start and end apart: 22, of which 16 were waited for; matrix products, arithmetic and copies ran while one was open for 13% of the time, Pallas kernels for 0%

commit v1 on v0

v1 whole, which is shorter than its diff:
```python
import functools
import math

import jax
import jax.numpy as jnp
from jax import lax
from jax.experimental import pallas as pl
from jax.experimental.pallas import tpu as pltpu
from jax.sharding import PartitionSpec as P

MESH = pl.DeviceIdType.MESH
F32 = jnp.float32
BF16 = jnp.bfloat16

LANES = 128
SLOTS = 32
SUBS = 4
LONG_CORE = 1.0
SHORT_CORE = 0.25
STEP = 0.05

ROWS_X = 24
ROWS_XLB = 72
ROWS_SETUP = 80
ROW_MOB = 72
ROW_F = 80
ROWS_ALL = 112


def take_lanes(rows, lane):
    return jnp.take_along_axis(rows, lane, axis=1, mode="promise_in_bounds")


def split3(value):
    high = value.astype(BF16)
    rest = value - high.astype(F32)
    mid = rest.astype(BF16)
    low = (rest - mid.astype(F32)).astype(BF16)
    return high.astype(F32), mid.astype(F32), low.astype(F32)


def kernel(
    n_blk,
    n_dom,
    pos_hbm,
    lin_hbm,
    bur_hbm,
    mob_hbm,
    clo_hbm,
    map_hbm,
    new_ref,
    vel_ref,
    pos_v,
    lin_v,
    bur_v,
    mob_v,
    state,
    far_blk,
    dom_in,
    force_in,
    merged,
    close,
    maps,
    map_all,
    feat,
    lhs,
    acc,
    statics_gh,
    weight_own,
    weight,
    ghost,
    frow,
    guess,
    xsend,
    xrecv,
    xx,
    local_sem,
    send_sem,
    recv_sem,
):
    me_b = lax.axis_index("blk")
    me_d = lax.axis_index("dom")

    def peer(db, dd):
        return {
            "blk": lax.rem(me_b + db + n_blk, n_blk),
            "dom": lax.rem(me_d + dd + n_dom, n_dom),
        }

    blk_steps = (1, -1, 2, -2)
    dom_steps = (-1, 1, -2, 2)

    local = []
    for i, (src, dst) in enumerate(
        (
            (pos_hbm, pos_v),
            (lin_hbm, lin_v),
            (bur_hbm, bur_v),
            (mob_hbm, mob_v),
            (clo_hbm, close.at[:, pl.ds(0, 1024)]),
            (map_hbm, maps.at[0]),
        )
    ):
        copy = pltpu.make_async_copy(src, dst, local_sem.at[i])
        copy.start()
        local.append(copy)

    barrier = pltpu.get_barrier_semaphore()
    for step in blk_steps:
        pl.semaphore_signal(barrier, inc=1, device_id=peer(step, 0), device_id_type=MESH)
    for step in dom_steps:
        pl.semaphore_signal(barrier, inc=1, device_id=peer(0, step), device_id_type=MESH)

    for copy in local[:4]:
        copy.wait()
    for first, ref in ((0, pos_v), (24, lin_v), (48, bur_v), (72, mob_v)):
        for k in range(ref.shape[0]):
            for q in range(8):
                state[pl.ds(first + k * 8 + q, 1), :] = ref[pl.ds(k, 1), pl.ds(q * LANES, LANES)]

    pl.semaphore_wait(barrier, 8)

    sends = []

    def send(src, dst, device):
        i = len(sends)
        copy = pltpu.make_async_remote_copy(
            src_ref=src,
            dst_ref=dst,
            send_sem=send_sem.at[i],
            recv_sem=recv_sem.at[i],
            device_id=device,
            device_id_type=MESH,
        )
        copy.start()
        sends.append(copy)
        return copy

    blk_copies = [
        send(state.at[pl.ds(0, ROWS_XLB)], far_blk.at[i], peer(step, 0))
        for i, step in enumerate(blk_steps)
    ]
    dom_copies = [
        send(
            state.at[pl.ds(0, ROWS_SETUP)],
            dom_in.at[i, pl.ds(0, ROWS_SETUP)],
            peer(0, step),
        )
        for i, step in enumerate(dom_steps)
    ]
    dom_copies += [
        send(map_hbm, maps.at[1 + i], peer(0, step)) for i, step in enumerate(dom_steps)
    ]
    dom_copies += [
        send(
            clo_hbm.at[:, pl.ds(i * 512, 512)],
            close.at[:, pl.ds(1024 + i * 512, 512)],
            peer(0, step),
        )
        for i, step in enumerate(dom_steps[:2])
    ]

    def centre(rows):
        return jnp.mean(rows, axis=1, keepdims=True)

    own_pos = [state[pl.ds(8 * k, 8), :] for k in range(3)]
    centres = [centre(rows) for rows in own_pos]
    one = jnp.ones((8, LANES), F32)
    zero = jnp.zeros((8, LANES), F32)

    def features(rows_of, target):
        pos = [rows_of(k) - centres[k] for k in range(3)]
        line = [rows_of(3 + k) for k in range(3)]
        burg = [rows_of(6 + k) for k in range(3)]
        square = pos[0] * pos[0] + pos[1] * pos[1] + pos[2] * pos[2]
        products = [b * l for b in burg for l in line]
        if target:
            rest = [-2.0 * p for p in pos] + [square, one, zero, zero]
        else:
            rest = pos + [one, square + LONG_CORE * LONG_CORE, zero, zero]
        return products + rest

    for f, value in enumerate(features(lambda k: state[pl.ds(8 * k, 8), :], True)):
        for piece, part in enumerate(split3(value)):
            feat[0, pl.ds((piece * 16 + f) * 8, 8), :] = part
    row16 = lax.broadcasted_iota(jnp.int32, (16, LANES), 0)
    numerator_row = row16 < 9

    def build(q, carry):
        part = [feat[0, pl.ds(piece * 128 + q, 16, stride=8), :] for piece in range(3)]
        order = (0, 0, 1, 0, 1, 2)
        for half in range(2):
            keep = numerator_row if half == 0 else jnp.logical_not(numerator_row)
            rows = jnp.concatenate(
                [jnp.where(keep, part[i], 0.0) for i in order]
                + [jnp.zeros((32, LANES), F32)],
                axis=0,
            )
            lhs[q, pl.ds(half * LANES, LANES), :] = rows.T.astype(BF16)
        return carry

    lax.fori_loop(0, 8, build, 0)

    def long_block(source_rows, s):
        for f, value in enumerate(features(source_rows, False)):
            for piece, part in enumerate(split3(value)):
                feat[0, pl.ds((piece * 16 + f) * 8, 8), :] = part
        for k in range(3):
            feat[1, pl.ds(8 * k, 8), :] = source_rows(k) - centres[k]

        def cell(q, carry):
            part = [feat[0, pl.ds(piece * 128 + q, 16, stride=8), :] for piece in range(3)]
            order = (0, 1, 0, 2, 1, 0)
            rhs = jnp.concatenate(
                [part[i] for i in order] + [jnp.zeros((32, LANES), F32)], axis=0
            ).astype(BF16)
            both = jnp.dot(lhs[q], rhs, preferred_element_type=F32)
            inverse = lax.rsqrt(both[LANES:])
            w = both[:LANES] * inverse * (inverse * inverse)
            for k in range(4):
                term = w if k == 3 else w * feat[1, pl.ds(8 * k + q, 1), :]
                if s == 0:
                    acc[q, k] = term
                else:
                    acc[q, k] += term
            return carry

        lax.fori_loop(0, 8, cell, 0)

    long_block(lambda k: state[pl.ds(8 * k, 8), :], 0)
    for i in range(4):
        blk_copies[i].wait_recv()
        long_block(lambda k: far_blk[i, pl.ds(8 * k, 8), :], i + 1)

    cell8 = lax.broadcasted_iota(jnp.int32, (8, LANES), 0)

    def reduce_cell(q, sums):
        pick = jnp.where(cell8 == q, 1.0, 0.0)
        return tuple(
            total
            + lax.dot_general(
                pick,
                acc[q, k],
                (((1,), (1,)), ((), ())),
                precision=lax.Precision.HIGHEST,
                preferred_element_type=F32,
            )
            for k, total in enumerate(sums)
        )

    sums = lax.fori_loop(0, 8, reduce_cell, (zero,) * 4)
    scale = 1.0 / math.sqrt(5 * LANES)
    for k in range(3):
        force = ((own_pos[k] - centres[k]) * sums[3] - sums[k]) * scale
        state[pl.ds(ROW_F + 8 * k, 8), :] = force
    force_copies = [
        send(state.at[pl.ds(ROW_F, 24)], force_in.at[i], peer(0, step))
        for i, step in enumerate(dom_steps[:2])
    ]

    for copy in local[4:]:
        copy.wait()
    for copy in dom_copies:
        copy.wait_recv()
    low_half = cell8 < 4
    for slot in range(5):
        for j in range(4):
            map_all[pl.ds((slot * 4 + j) * SUBS, SUBS), :] = maps[slot, :, pl.ds(j * LANES, LANES)]
    for k in range(10):
        rows = pl.ds(8 * k, 8)
        merged[0, rows, :] = jnp.where(low_half, dom_in[0, rows, :], dom_in[1, rows, :])
        merged[1, rows, :] = jnp.where(low_half, dom_in[2, rows, :], dom_in[3, rows, :])

    windows = []
    for slot_low, buf_low, slot_high, buf_high in ((2, 1, 1, 1), (0, 0, 3, 2), (4, 2, 0, 0)):
        for w in range(4):
            if w < 2:
                windows.append((buf_low, 4, slot_low, 256 + w * LANES))
            else:
                windows.append((buf_high, 0, slot_high, (w - 2) * LANES))

    def pick_window(tiles, index):
        lane = index & 127
        tile = (index >> 7) & 3
        rows = [take_lanes(t, lane) for t in tiles]
        low = jnp.where((tile & 1) == 0, rows[0], rows[1])
        high = jnp.where((tile & 1) == 0, rows[2], rows[3])
        return jnp.where(tile < 2, low, high)

    def map_rows(t, window):
        _, _, slot, first = window
        row = (slot * 4 + first // LANES) * SUBS + t
        return jnp.broadcast_to(map_all[pl.ds(row, 1), :], (8, LANES))

    def static_tile(buf, s):
        if buf == 0:
            return state[pl.ds(24 + s, 8, stride=8), :]
        return merged[buf - 1, pl.ds(24 + s, 8, stride=8), :]

    def own_row(e, k):
        return xx[pl.ds(k * 16 + e, 1), :]

    for k in range(6):
        xx[pl.ds(k * 16, 8), :] = state[pl.ds(24 + 8 * k, 8), :]
        xx[pl.ds(k * 16 + 8, 8), :] = merged[0, pl.ds(24 + 8 * k, 8), :]

    def dots(e, partner):
        line = (
            own_row(e, 0) * partner(0) + own_row(e, 1) * partner(1) + own_row(e, 2) * partner(2)
        )
        burg = (
            own_row(e, 3) * partner(3) + own_row(e, 4) * partner(4) + own_row(e, 5) * partner(5)
        )
        return line * burg

    def close_of(e):
        return close[:, pl.ds(pl.multiple_of(e * LANES, LANES), LANES)]

    def weights_own(e, carry):
        index = close_of(e)
        lane = index & 127

        def partner(k):
            return take_lanes(jnp.broadcast_to(own_row(e, k), (SLOTS, LANES)), lane)

        weight_own[e] = jnp.where(index < LANES, dots(e, partner), 0.0)
        return carry

    lax.fori_loop(0, 16, weights_own, 0)

    def window_of(e):
        return jnp.where(e < 8, lax.rem(e, 4), e - 4)

    def weights_ghost(t, carry):
        for w, window in enumerate(windows):
            buf, first, _, _ = window
            tiles = [static_tile(buf, first + i) for i in range(4)]
            statics_gh[pl.ds(w * 8, 8), :] = pick_window(tiles, map_rows(t, window))

        def one(e, carry):
            index = close_of(e)
            lane = index & 127
            base = window_of(e) * 8

            def partner(k):
                row = statics_gh[pl.ds(base + k, 1), :]
                return take_lanes(jnp.broadcast_to(row, (SLOTS, LANES)), lane)

            value = jnp.where(
                index < LANES,
                weight_own[e],
                jnp.where(index < 2 * LANES, dots(e, partner), 0.0),
            )
            weight[t, e] = value
            return carry

        lax.fori_loop(0, 16, one, 0)
        return carry

    lax.fori_loop(0, SUBS, weights_ghost, 0)

    def fill_ghosts(t, tile_of, count):
        for w, window in enumerate(windows[:count]):
            buf, first, _, _ = window
            tiles = [tile_of(buf, first + i) for i in range(4)]
            ghost[pl.ds(w * 8, 8), :] = pick_window(tiles, map_rows(t, window))

    def evaluate(t, rows, count):
        def one(e, carry):
            index = close_of(e)
            lane = index & 127
            is_ghost = (index & 128) != 0
            base = window_of(e) * 8
            deltas = []
            for k in range(3):
                own = rows[pl.ds(k * 16 + e, 1), :]
                other = ghost[pl.ds(base + k, 1), :]
                picked = jnp.where(
                    is_ghost,
                    take_lanes(jnp.broadcast_to(other, (SLOTS, LANES)), lane),
                    take_lanes(jnp.broadcast_to(own, (SLOTS, LANES)), lane),
                )
                deltas.append(own - picked)
            radius = (
                deltas[0] * deltas[0]
                + deltas[1] * deltas[1]
                + deltas[2] * deltas[2]
                + SHORT_CORE * SHORT_CORE
            )
            inverse = lax.rsqrt(radius)
            w = weight[t, e] * inverse * (inverse * inverse)
            for k in range(3):
                frow[pl.ds(k * 16 + e, 1), :] = jnp.sum(w * deltas[k], axis=0, keepdims=True)
            return carry

        lax.fori_loop(0, count, one, 0)

    short_scale = 1.0 / math.sqrt(SLOTS)
    mob_own = state[pl.ds(ROW_MOB, 8), :]
    mob_rim = merged[0, pl.ds(ROW_MOB, 8), :]

    for copy in force_copies:
        copy.wait_recv()
    for k in range(3):
        rows = pl.ds(8 * k, 8)
        merged[0, pl.ds(ROW_F + 8 * k, 8), :] = jnp.where(
            low_half, force_in[0, rows, :], force_in[1, rows, :]
        )

    for k in range(3):
        xx[pl.ds(k * 16, 8), :] = state[pl.ds(8 * k, 8), :]
        xx[pl.ds(k * 16 + 8, 8), :] = merged[0, pl.ds(8 * k, 8), :]
        guess[pl.ds(128 + k * 8, 8), :] = merged[1, pl.ds(8 * k, 8), :]

    def tile_now(buf, s):
        if buf == 2:
            return guess[pl.ds(128 + s, 8, stride=8), :]
        return xx[pl.ds(buf * 8 + s, 8, stride=16), :]

    def tile_guess(buf, s):
        return guess[pl.ds(buf * 8 + s, 8, stride=16), :]

    for t in range(SUBS):
        fill_ghosts(t, tile_now, 12)
        evaluate(t, xx, 16)
        firsts = []
        for k in range(3):
            for half, mob in ((0, mob_own), (1, mob_rim)):
                long_force = (
                    state[pl.ds(ROW_F + 8 * k, 8), :]
                    if half == 0
                    else merged[0, pl.ds(ROW_F + 8 * k, 8), :]
                )
                rows = pl.ds(k * 16 + half * 8, 8)
                first = mob * (long_force + frow[rows, :] * short_scale)
                guess[rows, :] = xx[rows, :] + STEP * first
                if half == 0:
                    firsts.append(first)
        fill_ghosts(t, tile_guess, 4)
        evaluate(t, guess, 8)
        for k in range(3):
            rows = pl.ds(k * 16, 8)
            second = mob_own * (
                state[pl.ds(ROW_F + 8 * k, 8), :] + frow[rows, :] * short_scale
            )
            velocity = 0.5 * (firsts[k] + second)
            position = xx[rows, :] + STEP * velocity
            if t < SUBS - 1:
                xsend[t, pl.ds(8 * k, 8), :] = position
                xx[rows, :] = position
            else:
                for q in range(8):
                    cols = pl.ds(q * LANES, LANES)
                    new_ref[pl.ds(k, 1), cols] = position[q : q + 1, :]
                    vel_ref[pl.ds(k, 1), cols] = velocity[q : q + 1, :]
        if t < SUBS - 1:
            copies = [
                send(xsend.at[t], xrecv.at[t, i], peer(0, step))
                for i, step in enumerate(dom_steps)
            ]
            for copy in copies:
                copy.wait_recv()
            for k in range(3):
                rows = pl.ds(8 * k, 8)
                xx[pl.ds(k * 16 + 8, 8), :] = jnp.where(
                    low_half, xrecv[t, 0, rows, :], xrecv[t, 1, rows, :]
                )
                guess[pl.ds(128 + k * 8, 8), :] = jnp.where(
                    low_half, xrecv[t, 2, rows, :], xrecv[t, 3, rows, :]
                )

    for copy in sends:
        copy.wait_send()


def solution(mesh):
    n_blk, n_dom = mesh.shape["blk"], mesh.shape["dom"]

    def step(positions, line_vectors, burgers, mobility, close_list, ghost_map):
        count = positions.shape[1]
        anywhere = pl.BlockSpec(memory_space=pl.ANY)
        vmem = pl.BlockSpec(memory_space=pltpu.VMEM)
        shape = jax.ShapeDtypeStruct((3, count), F32)
        n_sends = 4 + 4 + 4 + 2 + 2 + 4 * (SUBS - 1)
        return pl.pallas_call(
            functools.partial(kernel, n_blk, n_dom),
            out_shape=(shape, shape),
            in_specs=[anywhere] * 6,
            out_specs=(vmem, vmem),
            scratch_shapes=[
                pltpu.VMEM((3, count), F32),
                pltpu.VMEM((3, count), F32),
                pltpu.VMEM((3, count), F32),
                pltpu.VMEM((1, count), F32),
                pltpu.VMEM((ROWS_ALL, LANES), F32),
                pltpu.VMEM((4, ROWS_XLB, LANES), F32),
                pltpu.VMEM((4, ROWS_SETUP, LANES), F32),
                pltpu.VMEM((2, 24, LANES), F32),
                pltpu.VMEM((2, ROWS_ALL, LANES), F32),
                pltpu.VMEM((SLOTS, 2 * count), jnp.int32),
                pltpu.VMEM((5, SUBS, 512), jnp.int32),
                pltpu.VMEM((80, LANES), jnp.int32),
                pltpu.VMEM((2, 384, LANES), F32),
                pltpu.VMEM((8, 256, LANES), BF16),
                pltpu.VMEM((8, 4, LANES, LANES), F32),
                pltpu.VMEM((96, LANES), F32),
                pltpu.VMEM((16, SLOTS, LANES), F32),
                pltpu.VMEM((SUBS, 16, SLOTS, LANES), F32),
                pltpu.VMEM((96, LANES), F32),
                pltpu.VMEM((48, LANES), F32),
                pltpu.VMEM((192, LANES), F32),
                pltpu.VMEM((SUBS, 24, LANES), F32),
                pltpu.VMEM((SUBS, 4, 24, LANES), F32),
                pltpu.VMEM((128, LANES), F32),
                pltpu.SemaphoreType.DMA((6,)),
                pltpu.SemaphoreType.DMA((n_sends,)),
                pltpu.SemaphoreType.DMA((n_sends,)),
            ],
            compiler_params=pltpu.CompilerParams(collective_id=0, has_side_effects=True),
        )(positions, line_vectors, burgers, mobility.reshape(1, count), close_list, ghost_map)

    both = ("blk", "dom")
    return jax.shard_map(
        step,
        mesh=mesh,
        in_specs=(
            P(None, both),
            P(None, both),
            P(None, both),
            P(both),
            P(None, both),
            P(None, both),
        ),
        out_specs=(P(None, both), P(None, both)),
        check_vma=False,
    )
```

time: 1080 us -> 65.1 us (0.06)
  local copies, waits for them, and re-layouts: 964 us -> 1.94 us
  Pallas kernels: 0 us -> 62 us
  waiting for transfers between devices: 44.6 us -> 0 us
  starting transfers between devices: 43.1 us -> 0 us
  other arithmetic: 18.4 us -> 0 us
    gather x32 -> x0, local copies, waits for them, and re-layouts: 958 us -> none  [the longest x16 946 us: short_force(): jnp.take(extended_rows, places, axis=1, mode='fill', fill_value=0.0)]
    pallas_call x0 -> x1, Pallas kernels: none -> 62 us  [step(): pl.pallas_call(functools.partial(kernel, n_blk, n_dom), out_shape=(shape,...]
    ppermute x22 -> x0, waiting for transfers between devices: 44.6 us -> none  [the longest x9 33.6 us: extended(): lax.ppermute(head, axis, [((i + 1) % count, i) for i in range(count)])]
    ppermute x22 -> x0, starting transfers between devices: 43.1 us -> none  [the longest x9 29.4 us: extended(): lax.ppermute(head, axis, [((i + 1) % count, i) for i in range(count)])]
  transfers between devices with their start and end apart: 22 -> 0, of which waited for: 16 -> 0; matrix products, arithmetic and copies ran while one was open for 13% -> 0% of each run, Pallas kernels for 0% -> 0%
where the time goes in v1:
time: 65.1 us; the launch traced here: 64.6 us
  Pallas kernels  62 us (95%)
  local copies, waits for them, and re-layouts  1.94 us (3%)
    pallas_call x1, Pallas kernels, step(): pl.pallas_call(functools.partial(kernel, n_blk, n_dom), out_shape=(shape,...  62 us
    unnamed x4, local copies, waits for them, and re-layouts  1.94 us

profile of v1, /device:TPU:1, one launch (start us, length us, event | category | flops | bytes accessed | tf_op | source)
XLA Modules:
  0.0 64.6 jit_solution(5277866378768850060)
XLA Ops:
  0.6 62.0 %shard_map.77 = (f32[3,1024]{1,0:T(4,128)}, f32[3,1024]{1,0:T(4,128)}) custom-call(f32[3,1024]{1,0:T(4,128)} %pos_hbm.1, f32[3,1024]{1,0:T(4,128)} %lin_hbm.1, f32[3,1024]{1,0:T(4,128)} %bur_hbm.1, f32[1,1024]{1,0:T(1,128)} %bitcast.1, s32[32,1024]{1,0:T(8,128)} %clo_hbm.1, s32[4,512]{1,0:T(4,128)} %map_hbm.1), custom_call_target="tpu_custom_call" | custom-call | tf_op jit(solution)/shard_map/pallas_call | solution.py:485
  62.7 0.0 copy-start
  62.7 1.3 %copy.10 = f32[3,1024]{1,0:T(4,128)} copy(f32[3,1024]{1,0:T(4,128)} %get-tuple-element.4) | data formatting | bytes 24576
  64.0 0.0 copy-done
  64.0 0.6 copy.11
Async XLA Ops:
  62.7 1.3 %copy-start = (f32[3,1024]{1,0:T(4,128)S(1)}, f32[3,1024]{1,0:T(4,128)}, u32[]{:S(2)}) copy-start(f32[3,1024]{1,0:T(4,128)} %get-tuple-element.5) | copy-start | bytes 36868

commit v2 on v1

v2 whole, which is shorter than its diff:
```python
import functools
import math

import jax
import jax.numpy as jnp
from jax import lax
from jax.experimental import pallas as pl
from jax.experimental.pallas import tpu as pltpu
from jax.sharding import PartitionSpec as P

MESH = pl.DeviceIdType.MESH
F32 = jnp.float32
BF16 = jnp.bfloat16

LANES = 128
CELLS = 8
SLOTS = 32
SUBS = 4
LONG_CORE = 1.0
SHORT_CORE = 0.25
STEP = 0.05

ROWS_SETUP = 80
ROW_MOB = 72
ROW_F = 80
ROWS_ALL = 112

REACH = 4
OFFSETS = tuple(sign * k for k in range(1, REACH + 1) for sign in (1, -1))
BLK_STEPS = (1, -1, 2, -2)

G0, G1, G2, H1, G3, G4, H2 = range(7)
GROUPS_NEAR = {1: G1, 2: G2, 3: G3, 4: G4}
GROUPS_OUTER = {1: H1, 2: H2}
STAGE_GROUPS = (5, 3, 2, 1)
STAGE_DOMAINS = (7, 5, 3, 1)
DOMAINS = (0, 1, -1, 2, -2, 3, -3)


def slot_of(offset):
    return 2 * (abs(offset) - 1) + (offset < 0)


def upper_half(domain):
    if domain == 0:
        return G0
    return GROUPS_OUTER[domain] if domain > 0 else GROUPS_NEAR[-domain]


def lower_half(domain):
    if domain == 0:
        return G0
    return GROUPS_NEAR[domain] if domain > 0 else GROUPS_OUTER[-domain]


def windows_of(domain):
    result = []
    for w in range(4):
        near = domain - 1 if w < 2 else domain + 1
        group = upper_half(near) if w < 2 else lower_half(near)
        first = 4 if w < 2 else 0
        slot = 0 if near == 0 else 1 + slot_of(near)
        tile = 2 + w if w < 2 else w - 2
        served = []
        for half, cell in ((lower_half, w), (upper_half, 4 + w)):
            if abs(domain) in (0, 1) or half is (lower_half if domain > 0 else upper_half):
                served.append((half(domain), cell))
        result.append((group, first, slot, tile, served))
    return result


GATHER = lax.GatherDimensionNumbers(
    offset_dims=(),
    collapsed_slice_dims=(1,),
    start_index_map=(1,),
    operand_batching_dims=(0,),
    start_indices_batching_dims=(0,),
)


def take_lanes(rows, lane):
    return lax.gather(
        rows,
        lane[..., None],
        GATHER,
        slice_sizes=(1, 1),
        mode=lax.GatherScatterMode.PROMISE_IN_BOUNDS,
    )


def split3(value):
    high = value.astype(BF16)
    rest = value - high.astype(F32)
    mid = rest.astype(BF16)
    low = (rest - mid.astype(F32)).astype(BF16)
    return high.astype(F32), mid.astype(F32), low.astype(F32)


def fold_cells(parts, row):
    def join(a, b, mask, turn):
        return jnp.where(mask, a, b) + pltpu.roll(jnp.where(mask, b, a), turn, 0)

    def turned(start):
        return jnp.bitwise_and(row - start, 7)

    pairs = [join(parts[s], parts[s + 4], turned(s) < 4, 4) for s in range(4)]
    quads = [
        join(pairs[s], pairs[s + 2], jnp.bitwise_and(turned(s), 2) == 0, 6) for s in range(2)
    ]
    return join(quads[0], quads[1], jnp.bitwise_and(row, 1) == 0, 7)


def kernel(
    n_blk,
    n_dom,
    pos_hbm,
    lin_hbm,
    bur_hbm,
    mob_hbm,
    clo_hbm,
    map_hbm,
    new_ref,
    vel_ref,
    pos_v,
    lin_v,
    bur_v,
    mob_v,
    far_blk,
    dom_in,
    force_in,
    group,
    close,
    maps,
    map_all,
    feat,
    lhs,
    acc,
    statics_gh,
    weight_own,
    weight,
    ghost,
    frow,
    vfirst,
    xnow,
    xguess,
    xsend,
    xrecv,
    local_sem,
    send_sem,
    recv_sem,
):
    me_b = lax.axis_index("blk")
    me_d = lax.axis_index("dom")

    def peer(db, dd):
        return {
            "blk": lax.rem(me_b + db + n_blk, n_blk),
            "dom": lax.rem(me_d + dd + n_dom, n_dom),
        }

    local = []
    for i, (src, dst) in enumerate(
        (
            (pos_hbm, pos_v),
            (lin_hbm, lin_v),
            (bur_hbm, bur_v),
            (mob_hbm, mob_v),
            (clo_hbm, close.at[G0]),
            (map_hbm, maps.at[0]),
        )
    ):
        copy = pltpu.make_async_copy(src, dst, local_sem.at[i])
        copy.start()
        local.append(copy)

    barrier = pltpu.get_barrier_semaphore()
    for step in BLK_STEPS:
        pl.semaphore_signal(barrier, inc=1, device_id=peer(step, 0), device_id_type=MESH)
    for step in OFFSETS:
        pl.semaphore_signal(barrier, inc=1, device_id=peer(0, step), device_id_type=MESH)

    for copy in local[:4]:
        copy.wait()
    state = group.at[G0]
    for first, ref in ((0, pos_v), (24, lin_v), (48, bur_v), (72, mob_v)):
        for k in range(ref.shape[0]):
            for q in range(CELLS):
                state[pl.ds(first + k * 8 + q, 1), :] = ref[pl.ds(k, 1), pl.ds(q * LANES, LANES)]

    pl.semaphore_wait(barrier, len(BLK_STEPS) + len(OFFSETS))

    sends = []

    def send(src, dst, device):
        i = len(sends)
        copy = pltpu.make_async_remote_copy(
            src_ref=src,
            dst_ref=dst,
            send_sem=send_sem.at[i],
            recv_sem=recv_sem.at[i],
            device_id=device,
            device_id_type=MESH,
        )
        copy.start()
        sends.append(copy)
        return copy

    blk_copies = [
        send(state.at[pl.ds(0, 72)], far_blk.at[i], peer(step, 0))
        for i, step in enumerate(BLK_STEPS)
    ]
    dom_copies = []
    for offset in OFFSETS:
        dom_copies.append(
            send(
                state.at[pl.ds(0, ROWS_SETUP)],
                dom_in.at[slot_of(offset)],
                peer(0, -offset),
            )
        )
    for offset in OFFSETS:
        dom_copies.append(send(map_hbm, maps.at[1 + slot_of(offset)], peer(0, -offset)))
    for offset in OFFSETS[:6]:
        halves = (0, 1) if abs(offset) == 1 else ((0,) if offset > 0 else (1,))
        for half in halves:
            target = (lower_half, upper_half)[half](offset)
            cols = pl.ds(half * 512, 512)
            dom_copies.append(
                send(clo_hbm.at[:, cols], close.at[target, :, cols], peer(0, -offset))
            )

    own_pos = [state[pl.ds(8 * k, 8), :] for k in range(3)]
    centres = [jnp.mean(rows, axis=1, keepdims=True) for rows in own_pos]
    one = jnp.ones((8, LANES), F32)
    zero = jnp.zeros((8, LANES), F32)

    def put_features(rows_of, target):
        pos = [rows_of(k) - centres[k] for k in range(3)]
        line = [rows_of(3 + k) for k in range(3)]
        burg = [rows_of(6 + k) for k in range(3)]
        square = pos[0] * pos[0] + pos[1] * pos[1] + pos[2] * pos[2]
        products = [b * l for b in burg for l in line]
        if target:
            rest = [-2.0 * p for p in pos] + [square, one, zero, zero]
        else:
            rest = pos + [one, square + LONG_CORE * LONG_CORE, zero, zero]
            for k in range(3):
                feat[1, pl.ds(8 * k, 8), :] = pos[k]
        for f, value in enumerate(products + rest):
            for piece, part in enumerate(split3(value)):
                feat[0, pl.ds((piece * 16 + f) * 8, 8), :] = part

    put_features(lambda k: state[pl.ds(8 * k, 8), :], True)
    numerator_row = lax.broadcasted_iota(jnp.int32, (16, LANES), 0) < 9

    def build(q, carry):
        part = [feat[0, pl.ds(piece * 128 + q, 16, stride=8), :] for piece in range(3)]
        for half in range(2):
            keep = numerator_row if half == 0 else jnp.logical_not(numerator_row)
            rows = jnp.concatenate(
                [jnp.where(keep, part[i], 0.0) for i in (0, 0, 1, 0, 1, 2)]
                + [jnp.zeros((32, LANES), F32)],
                axis=0,
            )
            lhs[q, pl.ds(half * LANES, LANES), :] = rows.T.astype(BF16)
        return carry

    lax.fori_loop(0, CELLS, build, 0)

    def long_block(source_rows, s):
        put_features(source_rows, False)

        def cell(q, carry):
            part = [feat[0, pl.ds(piece * 128 + q, 16, stride=8), :] for piece in range(3)]
            rhs = jnp.concatenate(
                [part[i] for i in (0, 1, 0, 2, 1, 0)] + [jnp.zeros((32, LANES), F32)], axis=0
            ).astype(BF16)
            both = jnp.dot(lhs[q], rhs, preferred_element_type=F32)
            inverse = lax.rsqrt(both[LANES:])
            w = both[:LANES] * inverse * (inverse * inverse)
            for k in range(4):
                term = w if k == 3 else w * feat[1, pl.ds(8 * k + q, 1), :]
                if s == 0:
                    acc[q, k] = term
                else:
                    acc[q, k] += term
            return carry

        lax.fori_loop(0, CELLS, cell, 0, unroll=2)

    long_block(lambda k: state[pl.ds(8 * k, 8), :], 0)
    for i in range(4):
        blk_copies[i].wait_recv()
        long_block(lambda k: far_blk[i, pl.ds(8 * k, 8), :], i + 1)

    lane_id = lax.broadcasted_iota(jnp.int32, (LANES, LANES), 1)

    def reduce_cell(q, columns):
        for k in range(4):
            total = jnp.sum(acc[q, k], axis=1, keepdims=True)
            columns = jnp.where(lane_id == k * 8 + q, total, columns)
        return columns

    columns = lax.fori_loop(
        0, CELLS, reduce_cell, jnp.zeros((LANES, LANES), F32), unroll=2
    )
    sums = columns.T
    scale = 1.0 / math.sqrt(5 * LANES)
    for k in range(3):
        force = ((own_pos[k] - centres[k]) * sums[24:32] - sums[8 * k : 8 * k + 8]) * scale
        state[pl.ds(ROW_F + 8 * k, 8), :] = force
    force_copies = [
        send(state.at[pl.ds(ROW_F, 24)], force_in.at[slot_of(offset)], peer(0, -offset))
        for offset in OFFSETS[:6]
    ]

    row = lax.broadcasted_iota(jnp.int32, (8, LANES), 0)
    low_half = row < 4
    for copy in local[4:]:
        copy.wait()
    for copy in dom_copies:
        copy.wait_recv()

    def merge(source, rows, k, outer):
        above, below = source[slot_of(k), rows, :], source[slot_of(-k), rows, :]
        if outer:
            return jnp.where(low_half, below, above)
        return jnp.where(low_half, above, below)

    merged_groups = [(g, k, False) for k, g in GROUPS_NEAR.items()] + [
        (g, k, True) for k, g in GROUPS_OUTER.items()
    ]
    for g, k, outer in merged_groups:
        for c in range(10):
            rows = pl.ds(8 * c, 8)
            group[g, rows, :] = merge(dom_in, rows, k, outer)
    for slot in range(9):
        for j in range(4):
            map_all[pl.ds((slot * 4 + j) * SUBS, SUBS), :] = maps[slot, :, pl.ds(j * LANES, LANES)]
    for g in range(7):
        xnow[g, pl.ds(0, 24), :] = group[g, pl.ds(0, 24), :]

    def pick_windows(t, n_domains, n_groups, tile_of, target):
        for domain in DOMAINS[:n_domains]:
            for g, first, slot, tile, served in windows_of(domain):
                place = map_all[pl.ds((slot * 4 + tile) * SUBS + t, 1), :]
                place = jnp.broadcast_to(place, (8, LANES))
                lane = place & 127
                at = (place >> 7) & 3
                picked = [take_lanes(tile_of(g, first + i), lane) for i in range(4)]
                odd = (at & 1) != 0
                result = jnp.where(
                    at >= 2,
                    jnp.where(odd, picked[3], picked[2]),
                    jnp.where(odd, picked[1], picked[0]),
                )
                for g_to, cell in served:
                    if g_to < n_groups:
                        target[pl.ds((g_to * 8 + cell) * 8, 8), :] = result

    def spread(value):
        return jnp.broadcast_to(value, (8, LANES))

    def close_of(g, s, r):
        return close[g, pl.ds(8 * r, 8), pl.ds(s * LANES, LANES)]

    def dots(mine, other):
        line = mine[0] * other[0] + mine[1] * other[1] + mine[2] * other[2]
        burg = mine[3] * other[3] + mine[4] * other[4] + mine[5] * other[5]
        return line * burg

    def static_rows(g, s):
        return [spread(group[g, pl.ds(24 + 8 * k + s, 1), :]) for k in range(6)]

    def weights_own(g, carry):
        for s in range(CELLS):
            mine = static_rows(g, s)
            for r in range(4):
                index = close_of(g, s, r)
                lane = index & 127
                other = [take_lanes(m, lane) for m in mine]
                weight_own[g, s, pl.ds(8 * r, 8), :] = jnp.where(
                    index < LANES, dots(mine, other), 0.0
                )
        return carry

    lax.fori_loop(0, 5, weights_own, 0)

    def static_tile(g, s):
        return group[g, pl.ds(24 + s, 8, stride=8), :]

    def weights_ghost(t, n_domains, n_groups):
        pick_windows(t, n_domains, n_groups, static_tile, statics_gh)

        def one(g, carry):
            for s in range(CELLS):
                mine = static_rows(g, s)
                base = (g * 8 + s) * 8
                theirs = [spread(statics_gh[pl.ds(base + k, 1), :]) for k in range(6)]
                for r in range(4):
                    index = close_of(g, s, r)
                    lane = index & 127
                    other = [take_lanes(m, lane) for m in theirs]
                    value = jnp.where(index < 2 * LANES, dots(mine, other), 0.0)
                    rows = pl.ds(8 * r, 8)
                    weight[t, g, s, rows, :] = jnp.where(
                        index < LANES, weight_own[g, s, rows, :], value
                    )
            return carry

        lax.fori_loop(0, n_groups, one, 0)

    short_scale = 1.0 / math.sqrt(SLOTS)

    def tiles_in(positions):
        return lambda g, s: positions[g, pl.ds(s, 8, stride=8), :]

    def evaluate(t, stage, positions):
        n_groups = STAGE_GROUPS[stage]
        pick_windows(t, STAGE_DOMAINS[stage], n_groups, tiles_in(positions), ghost)

        def one(g, carry):
            sums = [[], [], []]
            for s in range(CELLS):
                mine = [spread(positions[g, pl.ds(8 * k + s, 1), :]) for k in range(3)]
                base = (g * 8 + s) * 8
                theirs = [spread(ghost[pl.ds(base + k, 1), :]) for k in range(3)]
                total = None
                for r in range(4):
                    index = close_of(g, s, r)
                    lane = index & 127
                    is_ghost = index >= LANES
                    inner = [take_lanes(m, lane) for m in mine]
                    outer = [take_lanes(m, lane) for m in theirs]
                    delta = [
                        m - jnp.where(is_ghost, o, i) for m, o, i in zip(mine, outer, inner)
                    ]
                    radius = (
                        delta[0] * delta[0]
                        + delta[1] * delta[1]
                        + delta[2] * delta[2]
                        + SHORT_CORE * SHORT_CORE
                    )
                    inverse = lax.rsqrt(radius)
                    w = weight[t, g, s, pl.ds(8 * r, 8), :] * inverse * (inverse * inverse)
                    terms = [w * d for d in delta]
                    total = terms if total is None else [a + b for a, b in zip(total, terms)]
                for k in range(3):
                    sums[k].append(total[k])
            for k in range(3):
                frow[g, pl.ds(8 * k, 8), :] = fold_cells(sums[k], row)
            return carry

        lax.fori_loop(0, n_groups, one, 0)

    def drift(g, k):
        rows = pl.ds(8 * k, 8)
        force = group[g, pl.ds(ROW_F + 8 * k, 8), :] + frow[g, rows, :] * short_scale
        return group[g, pl.ds(ROW_MOB, 8), :] * force

    def make_guess(n_groups):
        for g in range(n_groups):
            for k in range(3):
                rows = pl.ds(8 * k, 8)
                first = drift(g, k)
                vfirst[g, rows, :] = first
                xguess[g, rows, :] = xnow[g, rows, :] + STEP * first

    def advance(n_groups, last):
        for g in range(n_groups):
            for k in range(3):
                rows = pl.ds(8 * k, 8)
                velocity = 0.5 * (vfirst[g, rows, :] + drift(g, k))
                position = xnow[g, rows, :] + STEP * velocity
                if last:
                    for q in range(CELLS):
                        cols = pl.ds(q * LANES, LANES)
                        new_ref[pl.ds(k, 1), cols] = position[q : q + 1, :]
                        vel_ref[pl.ds(k, 1), cols] = velocity[q : q + 1, :]
                else:
                    xnow[g, rows, :] = position

    def finish_block(t, last):
        evaluate(t, 1, xguess)
        advance(3, False)
        evaluate(t + 1, 2, xnow)
        make_guess(2)
        evaluate(t + 1, 3, xguess)
        advance(1, last)

    weights_ghost(0, 7, 5)
    evaluate(0, 0, xnow)
    weights_ghost(1, 3, 2)
    for copy in force_copies:
        copy.wait_recv()
    for g, k, outer in ((G1, 1, False), (H1, 1, True), (G2, 2, False), (G3, 3, False)):
        for c in range(3):
            group[g, pl.ds(ROW_F + 8 * c, 8), :] = merge(force_in, pl.ds(8 * c, 8), k, outer)
    make_guess(5)
    finish_block(0, False)

    xsend[...] = xnow[G0, pl.ds(0, 24), :]
    x_copies = [
        send(xsend, xrecv.at[slot_of(offset)], peer(0, -offset)) for offset in OFFSETS
    ]
    weights_ghost(2, 7, 5)
    weights_ghost(3, 3, 2)
    for copy in x_copies:
        copy.wait_recv()
    for g, k, outer in merged_groups:
        for c in range(3):
            rows = pl.ds(8 * c, 8)
            xnow[g, rows, :] = merge(xrecv, rows, k, outer)
    evaluate(2, 0, xnow)
    make_guess(5)
    finish_block(2, True)

    for copy in sends:
        copy.wait_send()


def solution(mesh):
    n_blk, n_dom = mesh.shape["blk"], mesh.shape["dom"]

    def step(positions, line_vectors, burgers, mobility, close_list, ghost_map):
        count = positions.shape[1]
        anywhere = pl.BlockSpec(memory_space=pl.ANY)
        vmem = pl.BlockSpec(memory_space=pltpu.VMEM)
        shape = jax.ShapeDtypeStruct((3, count), F32)
        n_sends = 4 + 8 + 8 + 8 + 6 + 8
        return pl.pallas_call(
            functools.partial(kernel, n_blk, n_dom),
            out_shape=(shape, shape),
            in_specs=[anywhere] * 6,
            out_specs=(vmem, vmem),
            scratch_shapes=[
                pltpu.VMEM((3, count), F32),
                pltpu.VMEM((3, count), F32),
                pltpu.VMEM((3, count), F32),
                pltpu.VMEM((1, count), F32),
                pltpu.VMEM((4, 72, LANES), F32),
                pltpu.VMEM((8, ROWS_SETUP, LANES), F32),
                pltpu.VMEM((6, 24, LANES), F32),
                pltpu.VMEM((7, ROWS_ALL, LANES), F32),
                pltpu.VMEM((5, SLOTS, count), jnp.int32),
                pltpu.VMEM((9, SUBS, 512), jnp.int32),
                pltpu.VMEM((144, LANES), jnp.int32),
                pltpu.VMEM((2, 384, LANES), F32),
                pltpu.VMEM((CELLS, 256, LANES), BF16),
                pltpu.VMEM((CELLS, 4, LANES, LANES), F32),
                pltpu.VMEM((320, LANES), F32),
                pltpu.VMEM((5, CELLS, SLOTS, LANES), F32),
                pltpu.VMEM((SUBS, 5, CELLS, SLOTS, LANES), F32),
                pltpu.VMEM((320, LANES), F32),
                pltpu.VMEM((5, 24, LANES), F32),
                pltpu.VMEM((5, 24, LANES), F32),
                pltpu.VMEM((7, 64, LANES), F32),
                pltpu.VMEM((5, 64, LANES), F32),
                pltpu.VMEM((24, LANES), F32),
                pltpu.VMEM((8, 24, LANES), F32),
                pltpu.SemaphoreType.DMA((6,)),
                pltpu.SemaphoreType.DMA((n_sends,)),
                pltpu.SemaphoreType.DMA((n_sends,)),
            ],
            compiler_params=pltpu.CompilerParams(collective_id=0, has_side_effects=True),
        )(positions, line_vectors, burgers, mobility.reshape(1, count), close_list, ghost_map)

    both = ("blk", "dom")
    return jax.shard_map(
        step,
        mesh=mesh,
        in_specs=(
            P(None, both),
            P(None, both),
            P(None, both),
            P(both),
            P(None, both),
            P(None, both),
        ),
        out_specs=(P(None, both), P(None, both)),
        check_vma=False,
    )
```

time: 65.1 us -> 48.5 us (0.75)
  Pallas kernels: 62 us -> 45.8 us
    pallas_call x1, Pallas kernels: 62 us -> 45.8 us  [step(): pl.pallas_call(functools.partial(kernel, n_blk, n_dom), out_shape=(shape,...]
where the time goes in v2:
time: 48.5 us; the launch traced here: 48.4 us
  Pallas kernels  45.8 us (94%)
  local copies, waits for them, and re-layouts  1.94 us (4%)
  between operations  0.65 us (1%)
    pallas_call x1, Pallas kernels, step(): pl.pallas_call(functools.partial(kernel, n_blk, n_dom), out_shape=(shape,...  45.8 us
    unnamed x4, local copies, waits for them, and re-layouts  1.94 us

profile of v2, /device:TPU:1, one launch (start us, length us, event | category | flops | bytes accessed | tf_op | source)
XLA Modules:
  0.0 48.4 jit_solution(190945265759679334)
XLA Ops:
  0.6 45.8 %shard_map.77 = (f32[3,1024]{1,0:T(4,128)}, f32[3,1024]{1,0:T(4,128)}) custom-call(f32[3,1024]{1,0:T(4,128)} %pos_hbm.1, f32[3,1024]{1,0:T(4,128)} %lin_hbm.1, f32[3,1024]{1,0:T(4,128)} %bur_hbm.1, f32[1,1024]{1,0:T(1,128)} %bitcast.1, s32[32,1024]{1,0:T(8,128)} %clo_hbm.1, s32[4,512]{1,0:T(4,128)} %map_hbm.1), custom_call_target="tpu_custom_call" | custom-call | tf_op jit(solution)/shard_map/pallas_call | solution.py:531
  46.4 0.0 copy-start
  46.4 1.3 %copy.10 = f32[3,1024]{1,0:T(4,128)} copy(f32[3,1024]{1,0:T(4,128)} %get-tuple-element.4) | data formatting | bytes 24576
  47.8 0.0 copy-done
  47.8 0.6 %copy.11 = f32[3,1024]{1,0:T(4,128)} copy(f32[3,1024]{1,0:T(4,128)S(1)} %copy-done) | data formatting | bytes 24576
Async XLA Ops:
  46.4 1.3 %copy-start = (f32[3,1024]{1,0:T(4,128)S(1)}, f32[3,1024]{1,0:T(4,128)}, u32[]{:S(2)}) copy-start(f32[3,1024]{1,0:T(4,128)} %get-tuple-element.5) | copy-start | bytes 36868

commit v3 on v2

--- a/solution.py
+++ b/solution.py
@@ -32,8 +32,7 @@
 G0, G1, G2, H1, G3, G4, H2 = range(7)
 GROUPS_NEAR = {1: G1, 2: G2, 3: G3, 4: G4}
 GROUPS_OUTER = {1: H1, 2: H2}
-STAGE_GROUPS = (5, 3, 2, 1)
-STAGE_DOMAINS = (7, 5, 3, 1)
+DOMAINS_FOR = {1: 1, 2: 3, 3: 5, 5: 7}
 DOMAINS = (0, 1, -1, 2, -2, 3, -3)
 
 
@@ -119,15 +118,14 @@
     mob_hbm,
     clo_hbm,
     map_hbm,
-    new_ref,
-    vel_ref,
+    pos_out,
+    vel_out,
     pos_v,
     lin_v,
     bur_v,
     mob_v,
     far_blk,
     dom_in,
-    force_in,
     group,
     close,
     maps,
@@ -143,6 +141,9 @@
     vfirst,
     xnow,
     xguess,
+    xhalf,
+    msend,
+    mrecv,
     xsend,
     xrecv,
     local_sem,
@@ -209,25 +210,25 @@
         send(state.at[pl.ds(0, 72)], far_blk.at[i], peer(step, 0))
         for i, step in enumerate(BLK_STEPS)
     ]
-    dom_copies = []
-    for offset in OFFSETS:
-        dom_copies.append(
-            send(
-                state.at[pl.ds(0, ROWS_SETUP)],
-                dom_in.at[slot_of(offset)],
-                peer(0, -offset),
-            )
-        )
-    for offset in OFFSETS:
-        dom_copies.append(send(map_hbm, maps.at[1 + slot_of(offset)], peer(0, -offset)))
-    for offset in OFFSETS[:6]:
-        halves = (0, 1) if abs(offset) == 1 else ((0,) if offset > 0 else (1,))
-        for half in halves:
-            target = (lower_half, upper_half)[half](offset)
-            cols = pl.ds(half * 512, 512)
-            dom_copies.append(
-                send(clo_hbm.at[:, cols], close.at[target, :, cols], peer(0, -offset))
-            )
+
+    def send_state(k):
+        pairs = (k, -k)
+        return [
+            send(state.at[pl.ds(0, ROWS_SETUP)], dom_in.at[slot_of(o)], peer(0, -o)) for o in pairs
+        ] + [send(map_hbm, maps.at[1 + slot_of(o)], peer(0, -o)) for o in pairs]
+
+    def send_close(target, k, outer):
+        result = []
+        for o in (k, -k):
+            cols = pl.ds(512 * ((o > 0) == outer), 512)
+            result.append(send(clo_hbm.at[:, cols], close.at[target, :, cols], peer(0, -o)))
+        return result
+
+    copies_first = send_state(1)
+    copies_second = (
+        send_state(2) + send_close(G1, 1, False) + send_state(3) + send_close(G2, 2, False)
+    )
+    copies_third = send_close(H1, 1, True) + send_close(G3, 3, False) + send_state(4)
 
     own_pos = [state[pl.ds(8 * k, 8), :] for k in range(3)]
     centres = [jnp.mean(rows, axis=1, keepdims=True) for rows in own_pos]
@@ -289,37 +290,8 @@
         lax.fori_loop(0, CELLS, cell, 0, unroll=2)
 
     long_block(lambda k: state[pl.ds(8 * k, 8), :], 0)
-    for i in range(4):
-        blk_copies[i].wait_recv()
-        long_block(lambda k: far_blk[i, pl.ds(8 * k, 8), :], i + 1)
-
-    lane_id = lax.broadcasted_iota(jnp.int32, (LANES, LANES), 1)
-
-    def reduce_cell(q, columns):
-        for k in range(4):
-            total = jnp.sum(acc[q, k], axis=1, keepdims=True)
-            columns = jnp.where(lane_id == k * 8 + q, total, columns)
-        return columns
-
-    columns = lax.fori_loop(
-        0, CELLS, reduce_cell, jnp.zeros((LANES, LANES), F32), unroll=2
-    )
-    sums = columns.T
-    scale = 1.0 / math.sqrt(5 * LANES)
-    for k in range(3):
-        force = ((own_pos[k] - centres[k]) * sums[24:32] - sums[8 * k : 8 * k + 8]) * scale
-        state[pl.ds(ROW_F + 8 * k, 8), :] = force
-    force_copies = [
-        send(state.at[pl.ds(ROW_F, 24)], force_in.at[slot_of(offset)], peer(0, -offset))
-        for offset in OFFSETS[:6]
-    ]
-
     row = lax.broadcasted_iota(jnp.int32, (8, LANES), 0)
     low_half = row < 4
-    for copy in local[4:]:
-        copy.wait()
-    for copy in dom_copies:
-        copy.wait_recv()
 
     def merge(source, rows, k, outer):
         above, below = source[slot_of(k), rows, :], source[slot_of(-k), rows, :]
@@ -327,21 +299,25 @@
             return jnp.where(low_half, below, above)
         return jnp.where(low_half, above, below)
 
-    merged_groups = [(g, k, False) for k, g in GROUPS_NEAR.items()] + [
-        (g, k, True) for k, g in GROUPS_OUTER.items()
-    ]
-    for g, k, outer in merged_groups:
-        for c in range(10):
-            rows = pl.ds(8 * c, 8)
-            group[g, rows, :] = merge(dom_in, rows, k, outer)
-    for slot in range(9):
-        for j in range(4):
-            map_all[pl.ds((slot * 4 + j) * SUBS, SUBS), :] = maps[slot, :, pl.ds(j * LANES, LANES)]
-    for g in range(7):
-        xnow[g, pl.ds(0, 24), :] = group[g, pl.ds(0, 24), :]
-
-    def pick_windows(t, n_domains, n_groups, tile_of, target):
-        for domain in DOMAINS[:n_domains]:
+    near = {G1: (1, False), G2: (2, False), H1: (1, True), G3: (3, False), G4: (4, False), H2: (2, True)}
+
+    def merge_into(target, first, source, source_first, components, groups):
+        for g in groups:
+            k, outer = near[g]
+            for c in range(components):
+                target[g, pl.ds(first + 8 * c, 8), :] = merge(
+                    source, pl.ds(source_first + 8 * c, 8), k, outer
+                )
+
+    def put_maps(slots):
+        for slot in slots:
+            for j in range(4):
+                map_all[pl.ds((slot * 4 + j) * SUBS, SUBS), :] = maps[
+                    slot, :, pl.ds(j * LANES, LANES)
+                ]
+
+    def pick_windows(t, n_domains, n_groups, tile_of, target, start=0):
+        for domain in DOMAINS[start:n_domains]:
             for g, first, slot, tile, served in windows_of(domain):
                 place = map_all[pl.ds((slot * 4 + tile) * SUBS + t, 1), :]
                 place = jnp.broadcast_to(place, (8, LANES))
@@ -384,13 +360,11 @@
                 )
         return carry
 
-    lax.fori_loop(0, 5, weights_own, 0)
-
     def static_tile(g, s):
         return group[g, pl.ds(24 + s, 8, stride=8), :]
 
-    def weights_ghost(t, n_domains, n_groups):
-        pick_windows(t, n_domains, n_groups, static_tile, statics_gh)
+    def weights_ghost(t, n_groups, start=0):
+        pick_windows(t, DOMAINS_FOR[n_groups], n_groups, static_tile, statics_gh, start)
 
         def one(g, carry):
             for s in range(CELLS):
@@ -408,16 +382,15 @@
                     )
             return carry
 
-        lax.fori_loop(0, n_groups, one, 0)
+        lax.fori_loop(start, n_groups, one, 0)
 
     short_scale = 1.0 / math.sqrt(SLOTS)
 
     def tiles_in(positions):
         return lambda g, s: positions[g, pl.ds(s, 8, stride=8), :]
 
-    def evaluate(t, stage, positions):
-        n_groups = STAGE_GROUPS[stage]
-        pick_windows(t, STAGE_DOMAINS[stage], n_groups, tiles_in(positions), ghost)
+    def evaluate(t, n_groups, positions):
+        pick_windows(t, DOMAINS_FOR[n_groups], n_groups, tiles_in(positions), ghost)
 
         def one(g, carry):
             sums = [[], [], []]
@@ -463,57 +436,103 @@
             for k in range(3):
                 rows = pl.ds(8 * k, 8)
                 first = drift(g, k)
+                position = xnow[g, rows, :]
                 vfirst[g, rows, :] = first
-                xguess[g, rows, :] = xnow[g, rows, :] + STEP * first
-
-    def advance(n_groups, last):
+                xguess[g, rows, :] = position + STEP * first
+                xhalf[g, rows, :] = position + (0.5 * STEP) * first
+
+    def advance(n_groups):
         for g in range(n_groups):
             for k in range(3):
                 rows = pl.ds(8 * k, 8)
-                velocity = 0.5 * (vfirst[g, rows, :] + drift(g, k))
-                position = xnow[g, rows, :] + STEP * velocity
-                if last:
-                    for q in range(CELLS):
-                        cols = pl.ds(q * LANES, LANES)
-                        new_ref[pl.ds(k, 1), cols] = position[q : q + 1, :]
-                        vel_ref[pl.ds(k, 1), cols] = velocity[q : q + 1, :]
-                else:
-                    xnow[g, rows, :] = position
-
-    def finish_block(t, last):
-        evaluate(t, 1, xguess)
-        advance(3, False)
-        evaluate(t + 1, 2, xnow)
-        make_guess(2)
-        evaluate(t + 1, 3, xguess)
-        advance(1, last)
-
-    weights_ghost(0, 7, 5)
-    evaluate(0, 0, xnow)
-    weights_ghost(1, 3, 2)
-    for copy in force_copies:
+                xnow[g, rows, :] = xhalf[g, rows, :] + (0.5 * STEP) * drift(g, k)
+
+    for copy in local[4:]:
+        copy.wait()
+    lax.fori_loop(0, 1, weights_own, 0)
+    put_maps((0,))
+    for i in range(4):
+        blk_copies[i].wait_recv()
+        long_block(lambda k: far_blk[i, pl.ds(8 * k, 8), :], i + 1)
+
+    lane_id = lax.broadcasted_iota(jnp.int32, (LANES, LANES), 1)
+
+    def reduce_cell(q, columns):
+        for k in range(4):
+            total = jnp.sum(acc[q, k], axis=1, keepdims=True)
+            columns = jnp.where(lane_id == k * 8 + q, total, columns)
+        return columns
+
+    columns = lax.fori_loop(
+        0, CELLS, reduce_cell, jnp.zeros((LANES, LANES), F32), unroll=2
+    )
+    sums = columns.T
+    scale = 1.0 / math.sqrt(5 * LANES)
+    for k in range(3):
+        force = ((own_pos[k] - centres[k]) * sums[24:32] - sums[8 * k : 8 * k + 8]) * scale
+        state[pl.ds(ROW_F + 8 * k, 8), :] = force
+
+
+    for copy in copies_first:
         copy.wait_recv()
-    for g, k, outer in ((G1, 1, False), (H1, 1, True), (G2, 2, False), (G3, 3, False)):
-        for c in range(3):
-            group[g, pl.ds(ROW_F + 8 * c, 8), :] = merge(force_in, pl.ds(8 * c, 8), k, outer)
-    make_guess(5)
-    finish_block(0, False)
-
+    merge_into(group, 0, dom_in, 0, 10, (G1, H1))
+    put_maps((1, 2))
+    xnow[G0, pl.ds(0, 24), :] = state[pl.ds(0, 24), :]
+    xnow[G1, pl.ds(0, 24), :] = group[G1, pl.ds(0, 24), :]
+    weights_ghost(0, 1)
+    evaluate(0, 1, xnow)
+    make_guess(1)
+    for k in range(3):
+        for part, ref in ((0, xguess), (24, xhalf)):
+            msend[pl.ds(part + 8 * k, 8), :] = ref[G0, pl.ds(8 * k, 8), :]
+        msend[pl.ds(48 + 8 * k, 8), :] = group[G0, pl.ds(ROW_F + 8 * k, 8), :]
+    m_copies = [send(msend, mrecv.at[slot_of(o)], peer(0, -o)) for o in OFFSETS[:6]]
+
+    for copy in copies_second:
+        copy.wait_recv()
+    merge_into(group, 0, dom_in, 0, 10, (G2, G3, H2))
+    put_maps((3, 4, 5, 6))
+    lax.fori_loop(1, 3, weights_own, 0)
+    weights_ghost(0, 3, 1)
+    weights_ghost(1, 2)
+    for copy in m_copies:
+        copy.wait_recv()
+    merge_into(xguess, 0, mrecv, 0, 3, (G1, G2, H1, G3))
+    merge_into(xhalf, 0, mrecv, 24, 3, (G1, G2))
+    merge_into(group, ROW_F, mrecv, 48, 3, (G1, G2, H1, G3))
+    evaluate(0, 3, xguess)
+    advance(3)
+    evaluate(1, 2, xnow)
+    make_guess(2)
+    evaluate(1, 1, xguess)
+    advance(1)
     xsend[...] = xnow[G0, pl.ds(0, 24), :]
-    x_copies = [
-        send(xsend, xrecv.at[slot_of(offset)], peer(0, -offset)) for offset in OFFSETS
-    ]
-    weights_ghost(2, 7, 5)
-    weights_ghost(3, 3, 2)
+    x_copies = [send(xsend, xrecv.at[slot_of(o)], peer(0, -o)) for o in OFFSETS]
+
+    for copy in copies_third:
+        copy.wait_recv()
+    merge_into(group, 0, dom_in, 0, 10, (G4,))
+    put_maps((7, 8))
+    lax.fori_loop(3, 5, weights_own, 0)
+    weights_ghost(2, 5)
+    weights_ghost(3, 2)
     for copy in x_copies:
         copy.wait_recv()
-    for g, k, outer in merged_groups:
-        for c in range(3):
-            rows = pl.ds(8 * c, 8)
-            xnow[g, rows, :] = merge(xrecv, rows, k, outer)
-    evaluate(2, 0, xnow)
+    merge_into(xnow, 0, xrecv, 0, 3, (G1, G2, H1, G3, G4, H2))
+    evaluate(2, 5, xnow)
     make_guess(5)
-    finish_block(2, True)
+    evaluate(2, 3, xguess)
+    advance(3)
+    evaluate(3, 2, xnow)
+    make_guess(2)
+    evaluate(3, 1, xguess)
+    for k in range(3):
+        twice = vfirst[G0, pl.ds(8 * k, 8), :] + drift(G0, k)
+        position = xnow[G0, pl.ds(8 * k, 8), :]
+        for q in range(CELLS):
+            cols = pl.ds(q * LANES, LANES)
+            pos_out[pl.ds(k, 1), cols] = position[q : q + 1, :]
+            vel_out[pl.ds(k, 1), cols] = twice[q : q + 1, :]
 
     for copy in sends:
         copy.wait_send()
@@ -528,7 +547,7 @@
         vmem = pl.BlockSpec(memory_space=pltpu.VMEM)
         shape = jax.ShapeDtypeStruct((3, count), F32)
         n_sends = 4 + 8 + 8 + 8 + 6 + 8
-        return pl.pallas_call(
+        base, twice = pl.pallas_call(
             functools.partial(kernel, n_blk, n_dom),
             out_shape=(shape, shape),
             in_specs=[anywhere] * 6,
@@ -540,7 +559,6 @@
                 pltpu.VMEM((1, count), F32),
                 pltpu.VMEM((4, 72, LANES), F32),
                 pltpu.VMEM((8, ROWS_SETUP, LANES), F32),
-                pltpu.VMEM((6, 24, LANES), F32),
                 pltpu.VMEM((7, ROWS_ALL, LANES), F32),
                 pltpu.VMEM((5, SLOTS, count), jnp.int32),
                 pltpu.VMEM((9, SUBS, 512), jnp.int32),
@@ -556,6 +574,9 @@
                 pltpu.VMEM((5, 24, LANES), F32),
                 pltpu.VMEM((7, 64, LANES), F32),
                 pltpu.VMEM((5, 64, LANES), F32),
+                pltpu.VMEM((5, 24, LANES), F32),
+                pltpu.VMEM((72, LANES), F32),
+                pltpu.VMEM((6, 72, LANES), F32),
                 pltpu.VMEM((24, LANES), F32),
                 pltpu.VMEM((8, 24, LANES), F32),
                 pltpu.SemaphoreType.DMA((6,)),
@@ -564,6 +585,7 @@
             ],
             compiler_params=pltpu.CompilerParams(collective_id=0, has_side_effects=True),
         )(positions, line_vectors, burgers, mobility.reshape(1, count), close_list, ghost_map)
+        return base + (0.5 * STEP) * twice, 0.5 * twice
 
     both = ("blk", "dom")
     return jax.shard_map(

time: 48.5 us -> 43.9 us (0.905)
  Pallas kernels: 45.8 us -> 41.6 us
  local copies, waits for them, and re-layouts: 1.94 us -> 0 us
  other arithmetic: 0 us -> 1.35 us
    pallas_call x1, Pallas kernels: 45.8 us -> 41.6 us  [step(): pl.pallas_call(functools.partial(kernel, n_blk, n_dom), out_shape=(shape,...]
    unnamed x4 -> x0, local copies, waits for them, and re-layouts: 1.94 us -> none
    mul x0 -> x1, other arithmetic: none -> 1.35 us  [step(): return (base + 0.5 * STEP * twice, 0.5 * twice)]
where the time goes in v3:
time: 43.9 us; the launch traced here: 43.6 us
  Pallas kernels  41.6 us (95%)
  other arithmetic  1.35 us (3%)
  between operations  0.64 us (1%)
    pallas_call x1, Pallas kernels, step(): pl.pallas_call(functools.partial(kernel, n_blk, n_dom), out_shape=(shape,...  41.6 us
    mul x1, other arithmetic, step(): return (base + 0.5 * STEP * twice, 0.5 * twice)  1.35 us

profile of v3, /device:TPU:1, one launch (start us, length us, event | category | flops | bytes accessed | tf_op | source)
XLA Modules:
  0.0 43.6 jit_solution(4901980768933936736)
XLA Ops:
  0.6 41.6 %shard_map.77 = (f32[3,1024]{1,0:T(4,128)}, f32[3,1024]{1,0:T(4,128)}) custom-call(f32[3,1024]{1,0:T(4,128)} %pos_hbm.1, f32[3,1024]{1,0:T(4,128)} %lin_hbm.1, f32[3,1024]{1,0:T(4,128)} %bur_hbm.1, f32[1,1024]{1,0:T(1,128)} %bitcast.1, s32[32,1024]{1,0:T(8,128)} %clo_hbm.1, s32[4,512]{1,0:T(4,128)} %map_hbm.1), custom_call_target="tpu_custom_call" | custom-call | tf_op jit(solution)/shard_map/pallas_call | solution.py:550
  42.2 1.4 %broadcast_multiply_fusion = (f32[3,1024]{1,0:T(4,128)}, f32[3,1024]{1,0:T(4,128)}) fusion(f32[3,1024]{1,0:T(4,128)} %get-tuple-element.5, f32[3,1024]{1,0:T(4,128)} %get-tuple-element.4), kind=kLoop, calls=%fused_computation.1 | loop fusion | flops 9216 | bytes 49152 | tf_op jit(solution)/shard_map/mul | solution.py:588

commit v4 on v3

--- a/solution.py
+++ b/solution.py
@@ -14,6 +14,8 @@
 
 LANES = 128
 CELLS = 8
+PARTS = 4
+PART = 32
 SLOTS = 32
 SUBS = 4
 LONG_CORE = 1.0
@@ -131,6 +133,7 @@
     maps,
     map_all,
     feat,
+    feat_pos,
     lhs,
     acc,
     statics_gh,
@@ -228,14 +231,13 @@
     copies_second = (
         send_state(2) + send_close(G1, 1, False) + send_state(3) + send_close(G2, 2, False)
     )
-    copies_third = send_close(H1, 1, True) + send_close(G3, 3, False) + send_state(4)
 
     own_pos = [state[pl.ds(8 * k, 8), :] for k in range(3)]
     centres = [jnp.mean(rows, axis=1, keepdims=True) for rows in own_pos]
     one = jnp.ones((8, LANES), F32)
     zero = jnp.zeros((8, LANES), F32)
 
-    def put_features(rows_of, target):
+    def put_features(rows_of, target, at):
         pos = [rows_of(k) - centres[k] for k in range(3)]
         line = [rows_of(3 + k) for k in range(3)]
         burg = [rows_of(6 + k) for k in range(3)]
@@ -246,12 +248,12 @@
         else:
             rest = pos + [one, square + LONG_CORE * LONG_CORE, zero, zero]
             for k in range(3):
-                feat[1, pl.ds(8 * k, 8), :] = pos[k]
+                feat_pos[at, pl.ds(8 * k, 8), :] = pos[k]
         for f, value in enumerate(products + rest):
             for piece, part in enumerate(split3(value)):
-                feat[0, pl.ds((piece * 16 + f) * 8, 8), :] = part
-
-    put_features(lambda k: state[pl.ds(8 * k, 8), :], True)
+                feat[at, pl.ds((piece * 16 + f) * 8, 8), :] = part
+
+    put_features(lambda k: state[pl.ds(8 * k, 8), :], True, 0)
     numerator_row = lax.broadcasted_iota(jnp.int32, (16, LANES), 0) < 9
 
     def build(q, carry):
@@ -263,33 +265,47 @@
                 + [jnp.zeros((32, LANES), F32)],
                 axis=0,
             )
-            lhs[q, pl.ds(half * LANES, LANES), :] = rows.T.astype(BF16)
+            turned = rows.T.astype(BF16)
+            for part_at in range(PARTS):
+                lhs[q, pl.ds((2 * part_at + half) * PART, PART), :] = turned[
+                    part_at * PART : (part_at + 1) * PART
+                ]
         return carry
 
     lax.fori_loop(0, CELLS, build, 0)
 
-    def long_block(source_rows, s):
-        put_features(source_rows, False)
-
+    def long_blocks(count, first):
         def cell(q, carry):
-            part = [feat[0, pl.ds(piece * 128 + q, 16, stride=8), :] for piece in range(3)]
-            rhs = jnp.concatenate(
-                [part[i] for i in (0, 1, 0, 2, 1, 0)] + [jnp.zeros((32, LANES), F32)], axis=0
-            ).astype(BF16)
-            both = jnp.dot(lhs[q], rhs, preferred_element_type=F32)
-            inverse = lax.rsqrt(both[LANES:])
-            w = both[:LANES] * inverse * (inverse * inverse)
-            for k in range(4):
-                term = w if k == 3 else w * feat[1, pl.ds(8 * k + q, 1), :]
-                if s == 0:
-                    acc[q, k] = term
-                else:
-                    acc[q, k] += term
+            rhs = []
+            for s in range(count):
+                part = [feat[s, pl.ds(piece * 128 + q, 16, stride=8), :] for piece in range(3)]
+                rhs.append(
+                    jnp.concatenate(
+                        [part[i] for i in (0, 1, 0, 2, 1, 0)] + [jnp.zeros((32, LANES), F32)],
+                        axis=0,
+                    ).astype(BF16)
+                )
+            for part_at in range(PARTS):
+                rows = pl.ds(part_at * PART, PART)
+                total = None if first else [acc[q, k, rows, :] for k in range(4)]
+                for s in range(count):
+                    both = jnp.dot(
+                        lhs[q, pl.ds(2 * part_at * PART, 2 * PART), :],
+                        rhs[s],
+                        preferred_element_type=F32,
+                    )
+                    inverse = lax.rsqrt(both[PART:])
+                    w = both[:PART] * inverse * (inverse * inverse)
+                    terms = [w * feat_pos[s, pl.ds(8 * k + q, 1), :] for k in range(3)] + [w]
+                    total = terms if total is None else [a + b for a, b in zip(total, terms)]
+                for k in range(4):
+                    acc[q, k, rows, :] = total[k]
             return carry
 
         lax.fori_loop(0, CELLS, cell, 0, unroll=2)
 
-    long_block(lambda k: state[pl.ds(8 * k, 8), :], 0)
+    put_features(lambda k: state[pl.ds(8 * k, 8), :], False, 0)
+    long_blocks(1, True)
     row = lax.broadcasted_iota(jnp.int32, (8, LANES), 0)
     low_half = row < 4
 
@@ -453,7 +469,8 @@
     put_maps((0,))
     for i in range(4):
         blk_copies[i].wait_recv()
-        long_block(lambda k: far_blk[i, pl.ds(8 * k, 8), :], i + 1)
+        put_features(lambda k: far_blk[i, pl.ds(8 * k, 8), :], False, i)
+    long_blocks(4, False)
 
     lane_id = lax.broadcasted_iota(jnp.int32, (LANES, LANES), 1)
 
@@ -464,7 +481,7 @@
         return columns
 
     columns = lax.fori_loop(
-        0, CELLS, reduce_cell, jnp.zeros((LANES, LANES), F32), unroll=2
+        0, CELLS, reduce_cell, jnp.zeros((LANES, LANES), F32), unroll=4
     )
     sums = columns.T
     scale = 1.0 / math.sqrt(5 * LANES)
@@ -487,6 +504,7 @@
             msend[pl.ds(part + 8 * k, 8), :] = ref[G0, pl.ds(8 * k, 8), :]
         msend[pl.ds(48 + 8 * k, 8), :] = group[G0, pl.ds(ROW_F + 8 * k, 8), :]
     m_copies = [send(msend, mrecv.at[slot_of(o)], peer(0, -o)) for o in OFFSETS[:6]]
+    copies_third = send_close(H1, 1, True) + send_close(G3, 3, False) + send_state(4)
 
     for copy in copies_second:
         copy.wait_recv()
@@ -563,7 +581,8 @@
                 pltpu.VMEM((5, SLOTS, count), jnp.int32),
                 pltpu.VMEM((9, SUBS, 512), jnp.int32),
                 pltpu.VMEM((144, LANES), jnp.int32),
-                pltpu.VMEM((2, 384, LANES), F32),
+                pltpu.VMEM((4, 384, LANES), F32),
+                pltpu.VMEM((4, 24, LANES), F32),
                 pltpu.VMEM((CELLS, 256, LANES), BF16),
                 pltpu.VMEM((CELLS, 4, LANES, LANES), F32),
                 pltpu.VMEM((320, LANES), F32),

time: 43.9 us -> 41.1 us (0.936)
  Pallas kernels: 41.6 us -> 38.8 us
    pallas_call x1, Pallas kernels: 41.6 us -> 38.8 us  [step(): pl.pallas_call(functools.partial(kernel, n_blk, n_dom), out_shape=(shape,...]
where the time goes in v4:
time: 41.1 us; the launch traced here: 40.8 us
  Pallas kernels  38.8 us (94%)
  other arithmetic  1.35 us (3%)
  between operations  0.64 us (2%)
    pallas_call x1, Pallas kernels, step(): pl.pallas_call(functools.partial(kernel, n_blk, n_dom), out_shape=(shape,...  38.8 us
    mul x1, other arithmetic, step(): return (base + 0.5 * STEP * twice, 0.5 * twice)  1.35 us

profile of v4, /device:TPU:1, one launch (start us, length us, event | category | flops | bytes accessed | tf_op | source)
XLA Modules:
  0.0 40.8 jit_solution(2742440454084564940)
XLA Ops:
  0.6 38.8 %shard_map.77 = (f32[3,1024]{1,0:T(4,128)}, f32[3,1024]{1,0:T(4,128)}) custom-call(f32[3,1024]{1,0:T(4,128)} %pos_hbm.1, f32[3,1024]{1,0:T(4,128)} %lin_hbm.1, f32[3,1024]{1,0:T(4,128)} %bur_hbm.1, f32[1,1024]{1,0:T(1,128)} %bitcast.1, s32[32,1024]{1,0:T(8,128)} %clo_hbm.1, s32[4,512]{1,0:T(4,128)} %map_hbm.1), custom_call_target="tpu_custom_call" | custom-call | tf_op jit(solution)/shard_map/pallas_call | solution.py:568
  39.5 1.4 %broadcast_multiply_fusion = (f32[3,1024]{1,0:T(4,128)}, f32[3,1024]{1,0:T(4,128)}) fusion(f32[3,1024]{1,0:T(4,128)} %get-tuple-element.5, f32[3,1024]{1,0:T(4,128)} %get-tuple-element.4), kind=kLoop, calls=%fused_computation.1 | loop fusion | flops 9216 | bytes 49152 | tf_op jit(solution)/shard_map/mul | solution.py:607

commit v5 on v4

--- a/solution.py
+++ b/solution.py
@@ -214,7 +214,36 @@
         for i, step in enumerate(BLK_STEPS)
     ]
 
-    def send_state(k):
+    def landing(o, outer):
+        return 8 + (o < 0) if outer else slot_of(o)
+
+    def halves(ref, components, half):
+        view = ref.reshape(ref.shape[0] // 8, 8, LANES)
+        return view.at[components, pl.ds(4 * half, 4), :]
+
+    def send_maps(k, outer):
+        result = []
+        for o in (k, -k):
+            cols = pl.ds(256 * ((o > 0) == outer), 256)
+            result.append(
+                send(map_hbm.at[:, cols], maps.at[1 + landing(o, outer), :, cols], peer(0, -o))
+            )
+        return result
+
+    def send_statics(k, outer):
+        result = []
+        for o in (k, -k):
+            half = (o > 0) == outer
+            result.append(
+                send(
+                    halves(state, pl.ds(3, 7), half),
+                    halves(dom_in.at[landing(o, outer)], pl.ds(3, 7), half),
+                    peer(0, -o),
+                )
+            )
+        return result
+
+    def send_first(k):
         pairs = (k, -k)
         return [
             send(state.at[pl.ds(0, ROWS_SETUP)], dom_in.at[slot_of(o)], peer(0, -o)) for o in pairs
@@ -227,9 +256,14 @@
             result.append(send(clo_hbm.at[:, cols], close.at[target, :, cols], peer(0, -o)))
         return result
 
-    copies_first = send_state(1)
+    copies_first = send_first(1)
     copies_second = (
-        send_state(2) + send_close(G1, 1, False) + send_state(3) + send_close(G2, 2, False)
+        send_close(G1, 1, False)
+        + send_statics(2, False)
+        + send_maps(2, False)
+        + send_statics(3, False)
+        + send_maps(3, False)
+        + send_close(G2, 2, False)
     )
 
     own_pos = [state[pl.ds(8 * k, 8), :] for k in range(3)]
@@ -302,35 +336,39 @@
                     acc[q, k, rows, :] = total[k]
             return carry
 
-        lax.fori_loop(0, CELLS, cell, 0, unroll=2)
+        lax.fori_loop(0, CELLS, cell, 0, unroll=4)
 
     put_features(lambda k: state[pl.ds(8 * k, 8), :], False, 0)
     long_blocks(1, True)
     row = lax.broadcasted_iota(jnp.int32, (8, LANES), 0)
     low_half = row < 4
 
-    def merge(source, rows, k, outer):
-        above, below = source[slot_of(k), rows, :], source[slot_of(-k), rows, :]
+    def merge(source, rows, k, outer, first=None):
+        first = slot_of(k) if first is None else first
+        above, below = source[first, rows, :], source[first + 1, rows, :]
         if outer:
             return jnp.where(low_half, below, above)
         return jnp.where(low_half, above, below)
 
     near = {G1: (1, False), G2: (2, False), H1: (1, True), G3: (3, False), G4: (4, False), H2: (2, True)}
 
-    def merge_into(target, first, source, source_first, components, groups):
+    def merge_into(target, first, source, source_first, components, groups, slot=None):
         for g in groups:
             k, outer = near[g]
             for c in range(components):
                 target[g, pl.ds(first + 8 * c, 8), :] = merge(
-                    source, pl.ds(source_first + 8 * c, 8), k, outer
+                    source, pl.ds(source_first + 8 * c, 8), k, outer, slot
                 )
 
-    def put_maps(slots):
-        for slot in slots:
-            for j in range(4):
-                map_all[pl.ds((slot * 4 + j) * SUBS, SUBS), :] = maps[
-                    slot, :, pl.ds(j * LANES, LANES)
-                ]
+    def put_maps(source, slot, tiles):
+        for j in tiles:
+            map_all[pl.ds((slot * 4 + j) * SUBS, SUBS), :] = maps[
+                source, :, pl.ds(j * LANES, LANES)
+            ]
+
+    def put_near_maps(k):
+        put_maps(1 + slot_of(k), 1 + slot_of(k), (0, 1))
+        put_maps(1 + slot_of(-k), 1 + slot_of(-k), (2, 3))
 
     def pick_windows(t, n_domains, n_groups, tile_of, target, start=0):
         for domain in DOMAINS[start:n_domains]:
@@ -466,7 +504,7 @@
     for copy in local[4:]:
         copy.wait()
     lax.fori_loop(0, 1, weights_own, 0)
-    put_maps((0,))
+    put_maps(0, 0, range(4))
     for i in range(4):
         blk_copies[i].wait_recv()
         put_features(lambda k: far_blk[i, pl.ds(8 * k, 8), :], False, i)
@@ -481,7 +519,7 @@
         return columns
 
     columns = lax.fori_loop(
-        0, CELLS, reduce_cell, jnp.zeros((LANES, LANES), F32), unroll=4
+        0, CELLS, reduce_cell, jnp.zeros((LANES, LANES), F32), unroll=8
     )
     sums = columns.T
     scale = 1.0 / math.sqrt(5 * LANES)
@@ -493,31 +531,44 @@
     for copy in copies_first:
         copy.wait_recv()
     merge_into(group, 0, dom_in, 0, 10, (G1, H1))
-    put_maps((1, 2))
+    put_maps(1, 1, range(4))
+    put_maps(2, 2, range(4))
     xnow[G0, pl.ds(0, 24), :] = state[pl.ds(0, 24), :]
     xnow[G1, pl.ds(0, 24), :] = group[G1, pl.ds(0, 24), :]
     weights_ghost(0, 1)
     evaluate(0, 1, xnow)
     make_guess(1)
     for k in range(3):
-        for part, ref in ((0, xguess), (24, xhalf)):
+        for part, ref in ((0, xguess), (48, xhalf)):
             msend[pl.ds(part + 8 * k, 8), :] = ref[G0, pl.ds(8 * k, 8), :]
-        msend[pl.ds(48 + 8 * k, 8), :] = group[G0, pl.ds(ROW_F + 8 * k, 8), :]
-    m_copies = [send(msend, mrecv.at[slot_of(o)], peer(0, -o)) for o in OFFSETS[:6]]
-    copies_third = send_close(H1, 1, True) + send_close(G3, 3, False) + send_state(4)
+        msend[pl.ds(24 + 8 * k, 8), :] = group[G0, pl.ds(ROW_F + 8 * k, 8), :]
+    m_copies = [send(msend, mrecv.at[slot_of(o)], peer(0, -o)) for o in OFFSETS[:2]]
+    for k, count in ((2, 9), (3, 6)):
+        for o in (k, -k):
+            part = functools.partial(halves, components=pl.ds(0, count), half=o < 0)
+            m_copies.append(send(part(msend), part(mrecv.at[slot_of(o)]), peer(0, -o)))
+    copies_third = (
+        send_close(H1, 1, True)
+        + send_close(G3, 3, False)
+        + send_statics(2, True)
+        + send_maps(2, True)
+        + send_statics(4, False)
+        + send_maps(4, False)
+    )
 
     for copy in copies_second:
         copy.wait_recv()
-    merge_into(group, 0, dom_in, 0, 10, (G2, G3, H2))
-    put_maps((3, 4, 5, 6))
+    merge_into(group, 24, dom_in, 24, 7, (G2, G3))
+    put_near_maps(2)
+    put_near_maps(3)
     lax.fori_loop(1, 3, weights_own, 0)
     weights_ghost(0, 3, 1)
     weights_ghost(1, 2)
     for copy in m_copies:
         copy.wait_recv()
     merge_into(xguess, 0, mrecv, 0, 3, (G1, G2, H1, G3))
-    merge_into(xhalf, 0, mrecv, 24, 3, (G1, G2))
-    merge_into(group, ROW_F, mrecv, 48, 3, (G1, G2, H1, G3))
+    merge_into(xhalf, 0, mrecv, 48, 3, (G1, G2))
+    merge_into(group, ROW_F, mrecv, 24, 3, (G1, G2, H1, G3))
     evaluate(0, 3, xguess)
     advance(3)
     evaluate(1, 2, xnow)
@@ -525,12 +576,18 @@
     evaluate(1, 1, xguess)
     advance(1)
     xsend[...] = xnow[G0, pl.ds(0, 24), :]
-    x_copies = [send(xsend, xrecv.at[slot_of(o)], peer(0, -o)) for o in OFFSETS]
+    x_copies = [send(xsend, xrecv.at[slot_of(o)], peer(0, -o)) for o in OFFSETS[:4]]
+    for o in OFFSETS[4:]:
+        part = functools.partial(halves, components=pl.ds(0, 3), half=o < 0)
+        x_copies.append(send(part(xsend), part(xrecv.at[slot_of(o)]), peer(0, -o)))
 
     for copy in copies_third:
         copy.wait_recv()
-    merge_into(group, 0, dom_in, 0, 10, (G4,))
-    put_maps((7, 8))
+    merge_into(group, 24, dom_in, 24, 7, (G4,))
+    merge_into(group, 24, dom_in, 24, 7, (H2,), 8)
+    put_near_maps(4)
+    put_maps(9, 3, (2, 3))
+    put_maps(10, 4, (0, 1))
     lax.fori_loop(3, 5, weights_own, 0)
     weights_ghost(2, 5)
     weights_ghost(3, 2)
@@ -564,7 +621,7 @@
         anywhere = pl.BlockSpec(memory_space=pl.ANY)
         vmem = pl.BlockSpec(memory_space=pltpu.VMEM)
         shape = jax.ShapeDtypeStruct((3, count), F32)
-        n_sends = 4 + 8 + 8 + 8 + 6 + 8
+        n_sends = 4 + 4 + 12 + 12 + 6 + 8
         base, twice = pl.pallas_call(
             functools.partial(kernel, n_blk, n_dom),
             out_shape=(shape, shape),
@@ -576,10 +633,10 @@
                 pltpu.VMEM((3, count), F32),
                 pltpu.VMEM((1, count), F32),
                 pltpu.VMEM((4, 72, LANES), F32),
-                pltpu.VMEM((8, ROWS_SETUP, LANES), F32),
+                pltpu.VMEM((10, ROWS_SETUP, LANES), F32),
                 pltpu.VMEM((7, ROWS_ALL, LANES), F32),
                 pltpu.VMEM((5, SLOTS, count), jnp.int32),
-                pltpu.VMEM((9, SUBS, 512), jnp.int32),
+                pltpu.VMEM((11, SUBS, 512), jnp.int32),
                 pltpu.VMEM((144, LANES), jnp.int32),
                 pltpu.VMEM((4, 384, LANES), F32),
                 pltpu.VMEM((4, 24, LANES), F32),

time: 41.1 us -> 38.3 us (0.932)
  Pallas kernels: 38.8 us -> 36.1 us
    pallas_call x1, Pallas kernels: 38.8 us -> 36.1 us  [step(): pl.pallas_call(functools.partial(kernel, n_blk, n_dom), out_shape=(shape,...]
where the time goes in v5:
time: 38.3 us; the launch traced here: 38.1 us
  Pallas kernels  36.1 us (94%)
  other arithmetic  1.35 us (4%)
  between operations  0.64 us (2%)
    pallas_call x1, Pallas kernels, step(): pl.pallas_call(functools.partial(kernel, n_blk, n_dom), out_shape=(shape,...  36.1 us
    mul x1, other arithmetic, step(): return (base + 0.5 * STEP * twice, 0.5 * twice)  1.35 us

profile of v5, /device:TPU:1, one launch (start us, length us, event | category | flops | bytes accessed | tf_op | source)
XLA Modules:
  0.0 38.1 jit_solution(13894685528651468409)
XLA Ops:
  0.6 36.1 %shard_map.77 = (f32[3,1024]{1,0:T(4,128)}, f32[3,1024]{1,0:T(4,128)}) custom-call(f32[3,1024]{1,0:T(4,128)} %pos_hbm.1, f32[3,1024]{1,0:T(4,128)} %lin_hbm.1, f32[3,1024]{1,0:T(4,128)} %bur_hbm.1, f32[1,1024]{1,0:T(1,128)} %bitcast.1, s32[32,1024]{1,0:T(8,128)} %clo_hbm.1, s32[4,512]{1,0:T(4,128)} %map_hbm.1), custom_call_target="tpu_custom_call" | custom-call | tf_op jit(solution)/shard_map/pallas_call | solution.py:625
  36.7 1.4 %broadcast_multiply_fusion = (f32[3,1024]{1,0:T(4,128)}, f32[3,1024]{1,0:T(4,128)}) fusion(f32[3,1024]{1,0:T(4,128)} %get-tuple-element.5, f32[3,1024]{1,0:T(4,128)} %get-tuple-element.4), kind=kLoop, calls=%fused_computation.1 | loop fusion | flops 9216 | bytes 49152 | tf_op jit(solution)/shard_map/mul | solution.py:664

commit v6 on v5

--- a/solution.py
+++ b/solution.py
@@ -162,6 +162,12 @@
             "dom": lax.rem(me_d + dd + n_dom, n_dom),
         }
 
+    barrier = pltpu.get_barrier_semaphore()
+    for step in BLK_STEPS:
+        pl.semaphore_signal(barrier, inc=1, device_id=peer(step, 0), device_id_type=MESH)
+    for step in OFFSETS:
+        pl.semaphore_signal(barrier, inc=1, device_id=peer(0, step), device_id_type=MESH)
+
     local = []
     for i, (src, dst) in enumerate(
         (
@@ -176,12 +182,6 @@
         copy = pltpu.make_async_copy(src, dst, local_sem.at[i])
         copy.start()
         local.append(copy)
-
-    barrier = pltpu.get_barrier_semaphore()
-    for step in BLK_STEPS:
-        pl.semaphore_signal(barrier, inc=1, device_id=peer(step, 0), device_id_type=MESH)
-    for step in OFFSETS:
-        pl.semaphore_signal(barrier, inc=1, device_id=peer(0, step), device_id_type=MESH)
 
     for copy in local[:4]:
         copy.wait()
@@ -478,7 +478,7 @@
                 frow[g, pl.ds(8 * k, 8), :] = fold_cells(sums[k], row)
             return carry
 
-        lax.fori_loop(0, n_groups, one, 0)
+        lax.fori_loop(0, n_groups, one, 0, unroll=n_groups)
 
     def drift(g, k):
         rows = pl.ds(8 * k, 8)
@@ -542,11 +542,12 @@
         for part, ref in ((0, xguess), (48, xhalf)):
             msend[pl.ds(part + 8 * k, 8), :] = ref[G0, pl.ds(8 * k, 8), :]
         msend[pl.ds(24 + 8 * k, 8), :] = group[G0, pl.ds(ROW_F + 8 * k, 8), :]
-    m_copies = [send(msend, mrecv.at[slot_of(o)], peer(0, -o)) for o in OFFSETS[:2]]
-    for k, count in ((2, 9), (3, 6)):
+    m_copies = []
+    for k, count in ((3, 6), (2, 9)):
         for o in (k, -k):
             part = functools.partial(halves, components=pl.ds(0, count), half=o < 0)
             m_copies.append(send(part(msend), part(mrecv.at[slot_of(o)]), peer(0, -o)))
+    m_copies += [send(msend, mrecv.at[slot_of(o)], peer(0, -o)) for o in OFFSETS[:2]]
     copies_third = (
         send_close(H1, 1, True)
         + send_close(G3, 3, False)

time: 38.3 us -> 37 us (0.966)
  Pallas kernels: 36.1 us -> 34.7 us
    pallas_call x1, Pallas kernels: 36.1 us -> 34.7 us  [step(): pl.pallas_call(functools.partial(kernel, n_blk, n_dom), out_shape=(shape,...]
where the time goes in v6:
time: 37 us; the launch traced here: 36.7 us
  Pallas kernels  34.7 us (94%)
  other arithmetic  1.35 us (4%)
  between operations  0.64 us (2%)
    pallas_call x1, Pallas kernels, step(): pl.pallas_call(functools.partial(kernel, n_blk, n_dom), out_shape=(shape,...  34.7 us
    mul x1, other arithmetic, step(): return (base + 0.5 * STEP * twice, 0.5 * twice)  1.35 us

profile of v6, /device:TPU:1, one launch (start us, length us, event | category | flops | bytes accessed | tf_op | source)
XLA Modules:
  0.0 36.7 jit_solution(11994683159086823893)
XLA Ops:
  0.6 34.7 %shard_map.77 = (f32[3,1024]{1,0:T(4,128)}, f32[3,1024]{1,0:T(4,128)}) custom-call(f32[3,1024]{1,0:T(4,128)} %pos_hbm.1, f32[3,1024]{1,0:T(4,128)} %lin_hbm.1, f32[3,1024]{1,0:T(4,128)} %bur_hbm.1, f32[1,1024]{1,0:T(1,128)} %bitcast.1, s32[32,1024]{1,0:T(8,128)} %clo_hbm.1, s32[4,512]{1,0:T(4,128)} %map_hbm.1), custom_call_target="tpu_custom_call" | custom-call | tf_op jit(solution)/shard_map/pallas_call | solution.py:626
  35.4 1.4 %broadcast_multiply_fusion = (f32[3,1024]{1,0:T(4,128)}, f32[3,1024]{1,0:T(4,128)}) fusion(f32[3,1024]{1,0:T(4,128)} %get-tuple-element.5, f32[3,1024]{1,0:T(4,128)} %get-tuple-element.4), kind=kLoop, calls=%fused_computation.1 | loop fusion | flops 9216 | bytes 49152 | tf_op jit(solution)/shard_map/mul | solution.py:665
